TPU v7x, 128 devices: a whole 4x4x4 slice. The times are simulated.
128 devices in a mesh: strata: 8 (over y, core), chain: 16 (over z, x).
Axes of the slice: x: 4, y: 4, z: 4, core: 2. Of those that a mesh axis runs over, the one named last changes fastest.
Arguments:
- features: bfloat16 [262144, 512], P(('strata', 'chain')), may hold values from -6 to 6
- events: int32 [262144, 35], P(('strata', 'chain')), may hold values from 0 to 32767, as said below
- tie_first: int32 [262144], P(('strata', 'chain')), may hold values from 0 to 32767, as said below
- entry_row: int32 [262144], P(('strata', 'chain')), may hold values from 0 to 32767, as said below
- w_in: bfloat16 [512, 512], replicated, may hold values from -0.25 to 0.25
- w_mid: bfloat16 [512, 512], replicated, may hold values from -0.25 to 0.25
- w_out: bfloat16 [512, 512], replicated, may hold values from -0.25 to 0.25
Outputs:
- endpoint_loss: float32 [512], replicated
- grad_x: bfloat16 [262144, 512], P(('strata', 'chain'))
- grad_in: float32 [512, 512], replicated
- grad_mid: float32 [512, 512], replicated
- grad_out: float32 [512, 512], replicated
Inputs may be any that keep to these rules, and one draw needn't show every extreme that they name: Bit b of events[i, k] is row i's event indicator for endpoint 15 k + b; bits 15 and above, and bits for endpoints 512 and beyond, are zero. Groups of equal stop time are runs of consecutive rows lying inside aligned blocks of 2048 rows; tie_first[i] is the first row of row i's run, counted within its stratum. An interval is at risk at the stop time of row k's group exactly when entry_row <= tie_first[k] and the interval's row is >= tie_first[k]. For every row, tie_first[i] - 2048 < entry_row[i] <= tie_first[i]; in every aligned block of 2048 rows some row has entry_row = max(tie_first - 1 * 2048 + 1, 0).
All inputs are finite; a program needn't handle non-finite values.
Results may differ from a plain program's by a relative error of at most 0.006.
The roundings to bfloat16 on the way count: a program that leaves them out, or rounds other values in their place, can miss the bound.
Values sent between devices are 32-bit elements; how exact they have to be, the bound alone decides.
A program may use at most 128 MiB of HBM per device.

v0:
```python
import jax
import jax.numpy as jnp
from jax import lax
from jax.sharding import PartitionSpec as P

BACK = 1


def from_behind(block, axis, distance):
    devices = range(lax.axis_size(axis))
    route = [(i - distance, i) for i in devices if i - distance in devices]
    return lax.ppermute(block, axis, route)


def entering(x, axis, combine, identity, reverse):
    length, here = (lax.axis_size(axis), lax.axis_index(axis))
    everything = lax.all_gather(x, axis)
    start = jnp.broadcast_to(jnp.asarray(identity, x.dtype), x.shape)

    def hop(k, before):
        at = length - 1 - k if reverse else k
        reached = at > here if reverse else at < here
        new = combine(before, everything[at])
        return jnp.where(reached, new, before)

    return lax.fori_loop(0, length, hop, start)


def unpack_events(events, out_width):
    column = jnp.arange(out_width, dtype=jnp.int32)
    spread = jnp.repeat(events, 15, axis=1)[:, :out_width]
    return jnp.bitwise_and(jnp.right_shift(spread, column % 15), 1)


def silu_slope(value):
    sigma = jax.nn.sigmoid(value)
    return sigma * (1.0 + value * (1.0 - sigma))


def add_terms(earlier, latter):
    return earlier + latter


def on_device(features, events, tie_first, entry_row, w_in, w_mid, w_out):
    block_rows = features.shape[0]
    out_width = w_out.shape[1]
    chain_len = lax.axis_size("chain")
    position = lax.axis_index("chain")
    total_rows = block_rows * chain_len * lax.axis_size("strata")
    block_start = position * block_rows
    look_back = BACK
    window = (look_back + 1) * block_rows
    zero_row = jnp.zeros((out_width,), jnp.float32)
    preact = jnp.dot(features, w_in, preferred_element_type=jnp.float32)
    first_hidden = jax.nn.silu(preact).astype(jnp.bfloat16)
    mid_pre = jnp.dot(first_hidden, w_mid, preferred_element_type=jnp.float32)
    hidden = jax.nn.silu(mid_pre).astype(jnp.bfloat16)
    log_hazard = jnp.dot(hidden, w_out, preferred_element_type=jnp.float32)
    weight = jnp.exp(log_hazard)
    indicator = unpack_events(events, out_width).astype(jnp.float32)
    target = entry_row - (position - look_back) * block_rows
    landed = jax.ops.segment_sum(weight, target, num_segments=window)
    entered = landed[look_back * block_rows :]
    distance = 1
    portion = landed[(look_back - distance) * block_rows : (look_back - distance + 1) * block_rows]
    entered = entered + from_behind(portion, "chain", -distance)
    local_suffix = lax.cumsum(weight - entered, axis=0, reverse=True)
    beyond = entering(local_suffix[0], "chain", add_terms, zero_row, True)
    at_risk = beyond + local_suffix + entered
    local_first = tie_first - block_start
    divisor = jnp.take(at_risk, local_first, axis=0)
    loss_part = jnp.sum(indicator * (jnp.log(divisor) - log_hazard), axis=0) / total_rows
    hazard = indicator / divisor
    grouped = jax.ops.segment_sum(hazard, local_first, num_segments=block_rows)
    inclusive = lax.cumsum(grouped, axis=0)
    before = entering(inclusive[-1], "chain", add_terms, zero_row, False)
    own_block = before + inclusive - grouped
    blocks = [own_block]
    distance = 1
    blocks = [from_behind(own_block, "chain", distance)] + blocks
    stacked = jnp.concatenate(blocks, axis=0)
    exposure = before + inclusive - jnp.take(stacked, target, axis=0)
    eta_grad = (weight * exposure - indicator).astype(jnp.bfloat16)
    factor = total_rows ** (-0.5)
    grad_out = (
        jnp.einsum("rh,re->he", hidden, eta_grad, preferred_element_type=jnp.float32) * factor
    )
    hidden_grad = jnp.einsum("re,he->rh", eta_grad, w_out, preferred_element_type=jnp.float32)
    mid_grad = (hidden_grad * silu_slope(mid_pre)).astype(jnp.bfloat16)
    grad_mid = (
        jnp.einsum("rg,rh->gh", first_hidden, mid_grad, preferred_element_type=jnp.float32) * factor
    )
    first_grad = jnp.einsum("rh,gh->rg", mid_grad, w_mid, preferred_element_type=jnp.float32)
    pre_grad = (first_grad * silu_slope(preact)).astype(jnp.bfloat16)
    grad_in = (
        jnp.einsum("rf,rh->fh", features, pre_grad, preferred_element_type=jnp.float32) * factor
    )
    grad_x = jnp.einsum("rh,fh->rf", pre_grad, w_in, preferred_element_type=jnp.float32).astype(
        jnp.bfloat16
    )
    grad_in, grad_mid, grad_out, endpoint_loss = lax.psum(
        (grad_in, grad_mid, grad_out, loss_part), ("strata", "chain")
    )
    return (endpoint_loss, grad_x, grad_in, grad_mid, grad_out)


def solution(mesh):
    placed = (
        P(("strata", "chain"), None),
        P(("strata", "chain"), None),
        P(("strata", "chain")),
        P(("strata", "chain")),
        P(),
        P(),
        P(),
    )
    return jax.shard_map(
        on_device,
        mesh=mesh,
        in_specs=placed,
        out_specs=(P(), P(("strata", "chain"), None), P(), P(), P()),
        check_vma=False,
    )
```

profile of v0, /device:TPU:1, one launch (start us, length us, event | category | flops | bytes accessed | tf_op | source)
XLA Modules:
  0.0 558.4 jit_solution(1569800026435228325)
XLA Ops:
  8.8 4.8 multiply_convert_fusion.3
  13.6 3.8 multiply_convert_fusion.2
  20.7 17.5 %scatter_custom_fusion = f32[4096,512]{1,0:T(8,128)} fusion(s32[2048]{0:T(1024)S(1)} %get-tuple-element.261, f32[]{:T(128)} %constant.127.clone.1, f32[2048,512]{1,0:T(8,128)} %fusion.22), kind=kCustom, calls=%fused_computation.21 | custom fusion | flops 1048576 | bytes 12582916 | tf_op jit(solution)/shard_map/scatter-add | solution.py:62
  38.2 4.7 slice.42
  47.4 4.0 reshape.54
  51.5 4.7 slice.40
  56.2 5.4 copy.32
  61.6 75.5 %collective-permute-done = f32[2048,512]{1,0:T(8,128)} collective-permute-done((f32[2048,512]{1,0:T(8,128)}, f32[2048,512]{1,0:T(8,128)}, u32[]{:S(2)}, u32[]{:S(2)}) %collective-permute-start) | collective-permute-done | bytes 4194336 | tf_op jit(solution)/shard_map/ppermute | solution.py:12
  137.0 6.2 %exponential_subtract_fusion = f32[2048,512]{1,0:T(8,128)S(1)} fusion(f32[2048,512]{1,0:T(8,128)} %fusion.22, f32[2048,512]{1,0:T(8,128)} %collective-permute-done, f32[4096,512]{1,0:T(8,128)} %scatter_custom_fusion), kind=kLoop, calls=%fused_computation.31 | loop fusion | flops 2097152 | bytes 16777216 | tf_op jit(solution)/shard_map/sub | solution.py:67
  143.3 10.1 %fusion.2 = f32[512,16,128]{0,1,2:T(8,128)S(1)} fusion(f32[512,16,128]{0,2,1:T(8,128)S(1)} %bitcast.60), kind=kOutput, calls=%fused_computation.12 | output fusion | flops 133169152 | bytes 8388608 | tf_op jit(solution)/shard_map/reduce-window
  162.5 21.9 %all-gather = f32[16,1,512]{2,1,0:T(1,128)S(1)} all-gather(f32[1,1,512]{2,1,0:T(1,128)S(1)} %slice_bitcast_fusion.3), channel_id=1, replica_groups=mesh['strata'=8,'chain'=16] {'chain'}, dimensions={0}, use_global_device_ids=true | all-gather | bytes 34816 | tf_op jit(solution)/shard_map/all_gather | solution.py:17
  185.5 8.3 %add_add_fusion = f32[2048,512]{1,0:T(8,128)} fusion(f32[512]{0:T(512)S(1)} %get-tuple-element.194, f32[2048,512]{1,0:T(8,128)} %collective-permute-done, f32[4096,512]{1,0:T(8,128)} %scatter_custom_fusion, f32[512,16,128]{0,2,1:T(8,128)} %copy-done.4), kind=kLoop, calls=%fused_computation.20 | loop fusion | flops 3145728 | bytes 16779264 | tf_op jit(solution)/shard_map/add | solution.py:69
  193.7 11.7 %gather_fusion = f32[2048,512]{1,0:T(8,128)} fusion(f32[2048,512]{1,0:T(8,128)} %add_add_fusion, s32[2048]{0:T(1024)S(1)} %fusion.17), kind=kCustom, calls=%fused_computation | custom fusion | bytes 8396800 | tf_op jit(solution)/shard_map/jit(_take)/gather | solution.py:71
  205.5 17.3 %scatter_custom_fusion.1 = f32[2048,512]{1,0:T(8,128)} fusion(s32[2048]{0:T(1024)S(1)} %get-tuple-element.263, f32[2048,512]{1,0:T(8,128)} %gather_fusion, s32[2048,512]{1,0:T(8,128)} %copy.32, f32[]{:T(128)} %constant.127.clone.1, f32[]{:T(128)} %constant.130.clone.1, s32[]{:T(128)} %constant.123.clone.1, s32[512]{0:T(512)S(1)} %add_select_fusion.2, ...), kind=kCustom, calls=%fused_computation.17 | custom fusion | flops 6291456 | bytes 12587020 | tf_op jit(solution)/shard_map/scatter-add | solution.py:74
  222.8 4.6 fusion
  236.5 15.6 %all-gather.1 = f32[16,1,512]{2,1,0:T(1,128)S(1)} all-gather(f32[1,1,512]{2,1,0:T(1,128)S(1)} %slice_bitcast_fusion.2), channel_id=1, replica_groups=mesh['strata'=8,'chain'=16] {'chain'}, dimensions={0}, use_global_device_ids=true | all-gather | bytes 34816 | tf_op jit(solution)/shard_map/all_gather | solution.py:17
  253.0 4.5 add_subtract_fusion
  261.2 77.9 %collective-permute-done.1 = f32[2048,512]{1,0:T(8,128)S(1)} collective-permute-done((f32[2048,512]{1,0:T(8,128)S(1)}, f32[2048,512]{1,0:T(8,128)S(1)}, u32[]{:S(2)}, u32[]{:S(2)}) %collective-permute-start.1) | collective-permute-done | bytes 4194336 | tf_op jit(solution)/shard_map/ppermute | solution.py:12
  339.1 4.2 pad_maximum_fusion
  343.3 12.9 %gather_fusion.1 = f32[2048,512]{1,0:T(8,128)} fusion(f32[4096,512]{1,0:T(8,128)} %pad_maximum_fusion, s32[2048]{0:T(1024)S(1)} %fusion.18), kind=kCustom, calls=%fused_computation.1 | custom fusion | bytes 8396800 | tf_op jit(solution)/shard_map/jit(_take)/gather | solution.py:82
  356.2 8.5 %subtract_convert_fusion = (bf16[2048,512]{1,0:T(8,128)(2,1)S(1)}, f32[512]{0:T(512)S(1)}) fusion(f32[2048,512]{1,0:T(8,128)} %gather_fusion.1, f32[2048,512]{1,0:T(8,128)} %fusion.22, s32[2048,512]{1,0:T(8,128)} %copy.32, f32[512]{0:T(512)S(1)} %get-tuple-element.195, s32[512]{0:T(512)S(1)} %add_select_fusion.2, pred[2048]{0:T(1024)(128)(4,1)S(1)} %get-tuple-element.260, ...), kind=kLoop, calls=%fused_computation.16 | loop fusion | flops 13630976 | bytes 23078912 | tf_op jit(solution)/shard_map/convert_element_type | solution.py:83
  377.6 80.0 %psum.28 = f32[512]{0:T(512)} all-reduce(f32[512]{0:T(512)S(1)} %broadcast_multiply_fusion), channel_id=1, replica_groups=mesh['strata'=8,'chain'=16] {'strata','chain'}, use_global_device_ids=true, to_apply=%region_6.7 | all-reduce | flops 512 | bytes 4096 | tf_op jit(solution)/shard_map/psum | solution.py:101
  457.7 4.2 convolution_convert_fusion
  461.9 83.6 %all-reduce.3.cloned.1.call-done = (f32[512,512]{0,1:T(8,128)}, f32[512,512]{1,0:T(8,128)}, f32[512,512]{1,0:T(8,128)}) async-done(((f32[512,512]{0,1:T(8,128)}, f32[512,512]{1,0:T(8,128)}, f32[512,512]{1,0:T(8,128)}), (f32[512,512]{0,1:T(8,128)}, f32[512,512]{1,0:T(8,128)}, f32[512,512]{1,0:T(8,128)})) %all-reduce.3.cloned.1.call-update) | async-done | bytes 3145744 | tf_op jit(solution)/shard_map/psum | solution.py:101
  (138 shorter events, 52.6 us)
Async XLA Ops:
  7.2 1.6 copy-start
  7.2 538.3 %all-reduce.3.cloned.1.call-start = ((), (), s32[]{:S(2)}) async-start(), calls=%async_computation | async-start | bytes 6291456 | tf_op jit(solution)/shard_map/psum | solution.py:101
  8.8 4.8 copy-start.11
  13.6 3.8 copy-start.13
  13.6 3.8 copy-start.8
  17.4 3.3 copy-start.5
  38.2 6.6 %copy-start.9 = (s32[2048,35]{0,1:T(8,128)S(1)}, s32[2048,35]{0,1:T(8,128)}, u32[]{:S(2)}) copy-start(s32[2048,35]{0,1:T(8,128)} %param.12) | copy-start | bytes 860164
  42.9 94.1 %collective-permute-start = (f32[2048,512]{1,0:T(8,128)}, f32[2048,512]{1,0:T(8,128)}, u32[]{:S(2)}, u32[]{:S(2)}) collective-permute-start(f32[2048,512]{1,0:T(8,128)} %slice.42), channel_id=1, source_target_pairs={{1,0},{2,1},{3,2},{4,3},{5,4},{6,5},{7,6},{8,7},{9,8},{10,9},{11,1... | collective-permute-start | bytes 12582920 | tf_op jit(solution)/shard_map/ppermute | solution.py:12
  56.2 5.4 copy-start.10
  153.4 1.9 copy-start.2
  160.6 1.9 copy-start.4
  227.4 2.0 copy-start.3
  234.6 2.0 copy-start.1
  257.5 81.6 %collective-permute-start.1 = (f32[2048,512]{1,0:T(8,128)S(1)}, f32[2048,512]{1,0:T(8,128)S(1)}, u32[]{:S(2)}, u32[]{:S(2)}) collective-permute-start(f32[2048,512]{1,0:T(8,128)S(1)} %add_subtract_fusion), channel_id=1, source_target_pairs={{0,1},{1,2},{2,3},{3,4},{4,5},{5,6},{6,7},{7,8},{8,9},{9,10},{10,1... | collective-permute-start | bytes 12582920 | tf_op jit(solution)/shard_map/ppermute | solution.py:12
  356.2 8.5 %copy-start.6 = (bf16[2048,512]{1,0:T(8,128)(2,1)S(1)}, bf16[2048,512]{1,0:T(8,128)(2,1)}, u32[]{:S(2)}) copy-start(bf16[2048,512]{1,0:T(8,128)(2,1)} %copy-done.5) | copy-start | bytes 6291460
  364.7 2.3 copy-start.17
  367.0 2.4 copy-start.14
  369.4 2.3 copy-start.16
  374.0 1.3 copy-start.15
  375.3 82.3 %copy-start.12 = (bf16[512,512]{1,0:T(8,128)(2,1)S(1)}, bf16[512,512]{1,0:T(8,128)(2,1)}, u32[]{:S(2)}) copy-start(bf16[512,512]{1,0:T(8,128)(2,1)} %param.15) | copy-start | bytes 1572868
  545.5 4.9 copy-start.7
Sparse Core Ops, SparseCore 0:
  377.8 167.6 all-reduce.2
where the time goes:
time: 565 us; the launch traced here: 558 us
  waiting for transfers between devices  237 us (42%)
  blocking collectives  118 us (21%)
  other arithmetic  88.2 us (16%)
  local copies, waits for them, and re-layouts  67 us (12%)
  matrix products  27.6 us (5%)
  between operations  14.6 us (3%)
    ppermute x2, waiting for transfers between devices, from_behind(): return lax.ppermute(block, axis, route)  153 us
    psum x1, waiting for transfers between devices, on_device(): lax.psum((grad_in, grad_mid, grad_out, loss_part), ('strata', 'chain'))  83.6 us
    psum x1, blocking collectives, on_device(): lax.psum((grad_in, grad_mid, grad_out, loss_part), ('strata', 'chain'))  80 us
    all_gather x2, blocking collectives, entering(): everything = lax.all_gather(x, axis)  37.5 us
    unnamed x44, local copies, waits for them, and re-layouts  21.1 us
    scatter-add x1, other arithmetic, on_device(): landed = jax.ops.segment_sum(weight, target, num_segments=window)  17.5 us
    scatter-add x1, other arithmetic, on_device(): grouped = jax.ops.segment_sum(hazard, local_first, num_segments=block_rows)  17.3 us
    another operation x4, other arithmetic  14.9 us
  transfers between devices with their start and end apart: 3, of which 3 were waited for; matrix products, arithmetic and copies ran while one was open for 4% of the time, Pallas kernels for 0%

commit v1 on v0

v1 whole, which is shorter than its diff:
```python
import functools

import jax
import jax.numpy as jnp
import numpy as np
from jax import lax
from jax.experimental import pallas as pl
from jax.experimental.pallas import tpu as pltpu
from jax.sharding import PartitionSpec as P

T = 256
Q = 512
WORD_BITS = 15
F32 = jnp.float32
BF16 = jnp.bfloat16
I32 = jnp.int32
MESH = pl.DeviceIdType.MESH


def sigmoid(v):
    return 0.5 * jnp.tanh(0.5 * v) + 0.5


def span(i, size):
    return pl.ds(pl.multiple_of(i * size, size), size)


def dot(a, b, contract=((1,), (0,))):
    return lax.dot_general(a, b, (contract, ((), ())), preferred_element_type=F32)


def mask(build):
    return jnp.concatenate([jnp.where(build(h), 1.0, 0.0).astype(BF16) for h in range(Q // 128)], axis=1)


def unpack(words, table):
    hi = lax.shift_right_logical(words, 8).astype(F32).astype(BF16)
    lo = jnp.bitwise_and(words, 255).astype(F32).astype(BF16)
    value = dot(hi, table, ((0,), (0,))) * 256.0 + dot(lo, table, ((0,), (0,)))
    return value.astype(I32)


def coordinates():
    s, c = lax.axis_index("strata"), lax.axis_index("chain")
    return {"y": s // 2, "core": s % 2, "z": c // 4, "x": c % 4}


def device(at, **moved):
    at = {**at, **moved}
    return (at["y"] * 2 + at["core"], at["z"] * 4 + at["x"])


def reduce_all(given, factor, outs, loss_out, acc, pair, half, quarter, two, three, tally, send, recv, at, meanwhile):
    m = len(given)
    core = at["core"]
    half_rows = acc.shape[1]
    count = iter(range(send.shape[0]))
    flying = []

    def put(source, target, to):
        k = next(count)
        copy = pltpu.make_async_remote_copy(
            src_ref=source, dst_ref=target, send_sem=send.at[k], recv_sem=recv.at[k],
            device_id=to, device_id_type=MESH,
        )
        copy.start()
        flying.append(copy)
        return copy

    def rows(offset, size):
        return pl.ds(pl.multiple_of(offset, 8), size)

    class Stream:
        pass

    streams = []
    for t in range(m):
        s = Stream()
        s.t = t
        s.axes = ["xyz"[(t + k) % 3] for k in range(3)]
        p = at[s.axes[0]]
        high = p // 2
        low = (p + high) % 2
        s.near, s.far = (p // 2) * 2 + (1 - p % 2), 3 - p
        s.bits = [(low, high), (high, low)]
        s.partners = [(s.near, s.far), (s.far, s.near)]
        s.offset = [low * 64 + high * 32, 128 + high * 64 + low * 32]
        streams.append(s)

    axes_of_tally = ["core", "x", "y", "z"]

    def tally_send(k):
        axis = axes_of_tally[k]
        n = 2 if axis == "core" else 4
        return [
            put(tally.at[k, at[axis]], tally.at[k, at[axis]], device(at, **{axis: (at[axis] + d) % n}))
            for d in range(1, n)
        ]

    def tally_sum(k, copies):
        for copy in copies:
            copy.wait_recv()
        total = tally[k, 0]
        for slot in range(1, 2 if k == 0 else 4):
            total = total + tally[k, slot]
        return total

    tally_copies = tally_send(0)
    for s in streams:
        s.copies = [put(given[s.t].at[rows((1 - core) * half_rows, half_rows)], pair.at[s.t], device(at, core=1 - core))]
    meanwhile()
    for s in streams:
        s.copies[0].wait_recv()
        acc[s.t] = (given[s.t][rows(core * half_rows, half_rows), :] + pair[s.t]) * factor
        s.copies = []
        for u in range(2):
            away = 128 * u + (1 - s.bits[u][0]) * 64
            s.copies.append(put(acc.at[s.t, rows(away, 64)], half.at[s.t, u], device(at, **{s.axes[0]: s.partners[u][0]})))
    total = tally_sum(0, tally_copies)
    tally[1, at["x"]] = total
    tally_copies = tally_send(1)
    for s in streams:
        copies = []
        for u in range(2):
            s.copies[u].wait_recv()
            kept = rows(128 * u + s.bits[u][0] * 64, 64)
            acc[s.t, kept] = acc[s.t, kept] + half[s.t, u]
            away = 128 * u + s.bits[u][0] * 64 + (1 - s.bits[u][1]) * 32
            copies.append(put(acc.at[s.t, rows(away, 32)], quarter.at[s.t, u], device(at, **{s.axes[0]: s.partners[u][1]})))
        s.copies = copies
    total = tally_sum(1, tally_copies)
    tally[2, at["y"]] = total
    tally_copies = tally_send(2)
    for s in streams:
        q = at[s.axes[1]]
        copies = []
        for u in range(2):
            s.copies[u].wait_recv()
            kept = rows(s.offset[u], 32)
            acc[s.t, kept] = acc[s.t, kept] + quarter[s.t, u]
            for d in range(1, 4):
                to = (q + d) % 4
                copies.append(put(acc.at[s.t, rows(s.offset[u] + to * 8, 8)], two.at[s.t, q, pl.ds(u * 8, 8)],
                                  device(at, **{s.axes[1]: to})))
            two[s.t, q, u * 8 : u * 8 + 8] = acc[s.t, rows(s.offset[u] + q * 8, 8)]
        s.copies = copies
    total = tally_sum(2, tally_copies)
    tally[3, at["z"]] = total
    tally_copies = tally_send(3)
    for s in streams:
        r = at[s.axes[2]]
        for copy in s.copies:
            copy.wait_recv()
        three[s.t, r] = two[s.t, 0] + two[s.t, 1] + two[s.t, 2] + two[s.t, 3]
        s.copies = [put(three.at[s.t, r], three.at[s.t, r], device(at, **{s.axes[2]: (r + d) % 4})) for d in range(1, 4)]
    loss_out[...] = jnp.sum(tally_sum(3, tally_copies), axis=0, keepdims=True)
    base = core * half_rows
    for s in streams:
        q = at[s.axes[1]]
        for copy in s.copies:
            copy.wait_recv()
        final = three[s.t, 0] + three[s.t, 1] + three[s.t, 2] + three[s.t, 3]
        s.copies = []
        for u in range(2):
            piece = rows(base + s.offset[u] + q * 8, 8)
            outs[s.t][piece, :] = final[u * 8 : u * 8 + 8]
            for d in range(1, 4):
                s.copies.append(put(outs[s.t].at[piece], outs[s.t].at[piece], device(at, **{s.axes[1]: (q + d) % 4})))
    for s in streams:
        for copy in s.copies:
            copy.wait_recv()
        s.copies = []
        for u in range(2):
            piece = rows(base + s.offset[u], 32)
            s.copies.append(put(outs[s.t].at[piece], outs[s.t].at[piece], device(at, **{s.axes[0]: s.partners[u][1]})))
    for s in streams:
        copies = []
        for u in range(2):
            s.copies[u].wait_recv()
            piece = rows(base + 128 * u + s.bits[u][0] * 64, 64)
            copies.append(put(outs[s.t].at[piece], outs[s.t].at[piece], device(at, **{s.axes[0]: s.partners[u][0]})))
        s.copies = copies
    for s in streams:
        for copy in s.copies:
            copy.wait_recv()
        piece = rows(base, half_rows)
        s.copies = [put(outs[s.t].at[piece], outs[s.t].at[piece], device(at, core=1 - core))]
    for s in streams:
        s.copies[0].wait_recv()
    for copy in flying:
        copy.wait_send()


def step_kernel(
    x, evt, w_in, w_mid, w_out, spread, bit,
    gx_out, go_out, gm_out, gi_out, loss_out,
    fh, hid, s1, s2, ind, indp, wb, w, wn, wp, own, prev, hb, hp, nb, pb, first_col, firstp_col, entry_col,
    evp, idxn, logs, g, acc, pair, half, quarter, two, three, tally,
    small_send, small_recv, w_send, w_recv, gx_sem, send, recv, *, words, total_rows, chain,
):
    n, wide = x.shape[0], w_out.shape[1]
    parts, part = w.shape[0], w.shape[2]
    tiles, quarters = n // T, n // Q
    at = coordinates()
    me = lax.axis_index("chain")
    strata = lax.axis_index("strata")
    right, left = (strata, (me + 1) % chain), (strata, (me + chain - 1) % chain)

    barrier = pltpu.get_barrier_semaphore()
    friends = [left, right, device(at, core=1 - at["core"])]
    for axis in "xyz":
        friends += [device(at, **{axis: (at[axis] + d) % 4}) for d in range(1, 4)]
    for friend in friends:
        pl.semaphore_signal(barrier, inc=1, device_id=friend, device_id_type=MESH)
    pl.semaphore_wait(barrier, len(friends))

    def remote(source, target, s, r, to):
        return pltpu.make_async_remote_copy(
            src_ref=source, dst_ref=target, send_sem=s, recv_sem=r, device_id=to, device_id_type=MESH)

    top = words // 8 * 8
    ev_copy = remote(evt, evp, small_send.at[0], small_recv.at[0], right)
    id_copy = remote(evt.at[pl.ds(top, 8)], idxn, small_send.at[1], small_recv.at[1], left)
    ev_copy.start()
    id_copy.start()

    def to_left(c, r):
        rows = span(r, T)
        return remote(w.at[c, rows], wn.at[c, rows], w_send.at[0, c, r], w_recv.at[0, c, r], left)

    def to_right(c, r):
        rows = span(r, T)
        return remote(w.at[c, rows], wp.at[c, rows], w_send.at[1, c, r], w_recv.at[1, c, r], right)

    logs[...] = jnp.zeros_like(logs)

    def forward(r, _):
        rows = span(r, T)
        pre = dot(x[rows, :], w_in[...])
        s = sigmoid(pre)
        first = (pre * s).astype(BF16)
        fh[rows, :] = first
        s1[rows, :] = (s * (1.0 + pre * (1.0 - s))).astype(BF16)
        mid = dot(first, w_mid[...])
        s = sigmoid(mid)
        hidden = (mid * s).astype(BF16)
        hid[rows, :] = hidden
        s2[rows, :] = (s * (1.0 + mid * (1.0 - s))).astype(BF16)
        eta = dot(hidden, w_out[...])
        weight = jnp.exp(eta)
        for c in range(parts):
            w[c, rows, :] = weight[:, c * part : (c + 1) * part]
        to_left(0, r).start()
        to_right(0, r).start()
        wb[rows, :] = weight.astype(BF16)
        value = unpack(evt[:, rows], spread[...])
        flag = jnp.bitwise_and(lax.shift_right_logical(value[:, :wide], bit[...]), 1).astype(F32)
        ind[rows, :] = flag.astype(BF16)
        first_col[rows, :] = value[:, wide : wide + 128]
        entry_col[rows, :] = value[:, wide + 128 : wide + 256]
        logs[...] -= jnp.sum((flag * eta).reshape(-1, 8, wide), axis=0)
        return 0

    lax.fori_loop(0, tiles, forward, 0)

    def later(r, _):
        for c in range(1, parts):
            to_left(c, r).start()
            to_right(c, r).start()
        return 0

    lax.fori_loop(0, tiles, later, 0)

    ev_copy.wait_recv()
    id_copy.wait_recv()
    real = jnp.where(me > 0, 1.0, 0.0).astype(F32)
    idxn[...] = idxn[...] + jnp.where(me == chain - 1, 1 << 20, 0)

    def unpack_prev(r, _):
        rows = span(r, T)
        value = unpack(evp[:, rows], spread[...])
        flag = jnp.bitwise_and(lax.shift_right_logical(value[:, :wide], bit[...]), 1).astype(F32)
        indp[rows, :] = (flag * real).astype(BF16)
        firstp_col[rows, :] = value[:, wide : wide + 128]
        return 0

    lax.fori_loop(0, tiles, unpack_prev, 0)

    def lane(base):
        return lax.broadcasted_iota(I32, (Q, 128), 1) + base

    def row(table, k, j, h):
        return table[k : k + 1, j * Q + h * 128 : j * Q + (h + 1) * 128]

    FIRST, ENTRY, ENTRY_N = words, words + 1, words + 1 - top

    def own_part(i, _):
        rows = span(i, Q)
        first, firstp = first_col[rows, :], firstp_col[rows, :]
        total = totalp = 0.0
        for j in range(quarters):
            m = mask(lambda h: (row(evt, ENTRY, j, h) <= first + n) & (first <= lane(j * Q + h * 128)))
            total += dot(m, wb[j * Q : (j + 1) * Q, :])
        for c in range(parts):
            own[c, rows, :] = total[:, c * part : (c + 1) * part]
        for j in range(quarters):
            m = mask(lambda h: row(evt, ENTRY, j, h) <= firstp)
            totalp += dot(m, wb[j * Q : (j + 1) * Q, :])
        for c in range(parts):
            prev[c, rows, :] = totalp[:, c * part : (c + 1) * part]
        return 0

    lax.fori_loop(0, quarters, own_part, 0)

    eta_ref = wb
    for c in range(parts):
        cols = slice(c * part, (c + 1) * part)
        for q in range(quarters):
            for r in range(q * Q // T, (q + 1) * Q // T):
                to_left(c, r).wait_recv()
                to_right(c, r).wait_recv()
            nb[...] = wn[c, q * Q : (q + 1) * Q, :].astype(BF16)
            pb[...] = wp[c, q * Q : (q + 1) * Q, :].astype(BF16)

            def arrive(i, _):
                rows = span(i, Q)
                first, firstp = first_col[rows, :], firstp_col[rows, :]
                own[c, rows, :] += dot(mask(lambda h: row(idxn, ENTRY_N, q, h) <= first), nb[...])
                m = mask(lambda h: (row(evp, ENTRY, q, h) <= firstp + n) & (firstp <= lane(q * Q + h * 128)))
                prev[c, rows, :] += dot(m, pb[...])
                return 0

            lax.fori_loop(0, quarters, arrive, 0)

        def hazards(i, _):
            rows = span(i, T)
            divisor = own[c, rows, :]
            flag = ind[rows, cols].astype(F32) > 0.0
            hb[rows, :] = jnp.where(flag, 1.0 / divisor, 0.0).astype(BF16)
            log = jnp.where(flag, jnp.log(divisor), 0.0)
            logs[:, cols] += jnp.sum(log.reshape(-1, 8, part), axis=0)
            flagp = indp[rows, cols].astype(F32) > 0.0
            hp[rows, :] = jnp.where(flagp, 1.0 / prev[c, rows, :], 0.0).astype(BF16)
            return 0

        lax.fori_loop(0, tiles, hazards, 0)

        def expose(j, _):
            rows = span(j, Q)
            entry = entry_col[rows, :]
            here = lax.broadcasted_iota(I32, (Q, 128), 0) + j * Q
            total = 0.0
            for i in range(quarters):
                block = slice(i * Q, (i + 1) * Q)
                m = mask(lambda h: (entry <= row(evt, FIRST, i, h) + n) & (row(evt, FIRST, i, h) <= here))
                total += dot(m, hb[block, :])
                total += dot(mask(lambda h: entry <= row(evp, FIRST, i, h)), hp[block, :])
            eta_ref[rows, cols] = (w[c, rows, :] * total - ind[rows, cols].astype(F32)).astype(BF16)
            return 0

        lax.fori_loop(0, quarters, expose, 0)
        g[0, :, cols] = dot(hid[...], eta_ref[:, cols], ((0,), (0,)))

    pre_ref = s1

    def backward(i, _):
        rows = span(i, Q)
        mid_grad = (dot(eta_ref[rows, :], w_out[...], ((1,), (1,))) * s2[rows, :].astype(F32)).astype(BF16)
        pre_grad = (dot(mid_grad, w_mid[...], ((1,), (1,))) * s1[rows, :].astype(F32)).astype(BF16)
        pre_ref[rows, :] = pre_grad
        gm, gi = dot(fh[rows, :], mid_grad, ((0,), (0,))), dot(x[rows, :], pre_grad, ((0,), (0,)))

        @pl.when(i == 0)
        def _():
            g[1], g[2] = gm, gi

        @pl.when(i > 0)
        def _():
            g[1] += gm
            g[2] += gi

        return 0

    lax.fori_loop(0, quarters, backward, 0)

    tally[0, at["core"]] = logs[...] / total_rows

    def inputs_gradient():
        def tile(i, _):
            rows = span(i, Q)
            fh[rows, :] = dot(pre_ref[rows, :], w_in[...], ((1,), (1,))).astype(BF16)
            return 0

        lax.fori_loop(0, quarters, tile, 0)
        pltpu.make_async_copy(fh, gx_out, gx_sem).start()

    reduce_all([g.at[0], g.at[1], g.at[2]], total_rows ** (-0.5), [go_out, gm_out, gi_out], loss_out,
               acc, pair, half, quarter, two, three, tally, send, recv, at, inputs_gradient)
    pltpu.make_async_copy(fh, gx_out, gx_sem).wait()
    ev_copy.wait_send()
    id_copy.wait_send()

    def drain(r, _):
        for c in range(parts):
            to_left(c, r).wait_send()
            to_right(c, r).wait_send()
        return 0

    lax.fori_loop(0, tiles, drain, 0)


def on_device(features, events, tie_first, entry_row, w_in, w_mid, w_out):
    n, width = features.shape
    hidden_width, wide = w_out.shape
    words = events.shape[1]
    chain, strata = lax.axis_size("chain"), lax.axis_size("strata")
    assert (width, hidden_width, wide, n % Q) == (512, 512, 512, 0) and words % 8 in range(1, 7)
    parts = 2
    part = wide // parts
    start = lax.axis_index("chain") * n
    deep = words // 8 * 8 + 8
    evt = jnp.concatenate([
        events.T, (tie_first - start)[None], (entry_row - start + n)[None],
        jnp.zeros((deep - words - 2, n), I32)])
    column = np.arange(wide + 256)
    source = np.where(column < wide, column // WORD_BITS, words + (column - wide) // 128)
    spread = jnp.asarray((source[None, :] == np.arange(deep)[:, None]).astype(np.float32), BF16)
    bit = jnp.asarray((np.arange(wide) % WORD_BITS)[None, :].astype(np.int32))

    m = 3
    half_rows = hidden_width // 2
    messages = m * 25 + 10
    V = pltpu.VMEM
    dma = pltpu.SemaphoreType.DMA
    whole = V((n, wide), BF16)
    scratch = (
        [whole] * 7
        + [V((parts, n, part), F32)] * 5
        + [V((n, part), BF16)] * 2 + [V((Q, part), BF16)] * 2 + [V((n, 128), I32)] * 3
        + [V((deep, n), I32), V((8, n), I32), V((8, wide), F32), V((m, hidden_width, wide), F32)]
        + [V((m, half_rows, wide), F32)] * 2
        + [V((m, 2, 64, wide), F32), V((m, 2, 32, wide), F32), V((m, 4, 16, wide), F32), V((m, 4, 16, wide), F32),
           V((4, 4, 8, wide), F32)]
        + [dma((2,))] * 2 + [dma((2, parts, n // T))] * 2 + [dma, dma((messages,)), dma((messages,))]
    )
    vmem = pl.BlockSpec(memory_space=V)
    grad = jax.ShapeDtypeStruct((hidden_width, wide), F32)
    gx, go, gm, gi, loss = pl.pallas_call(
        functools.partial(step_kernel, words=words, total_rows=n * chain * strata, chain=chain),
        in_specs=[vmem] * 7,
        out_specs=[pl.BlockSpec(memory_space=pl.ANY)] + [vmem] * 4,
        out_shape=[jax.ShapeDtypeStruct((n, width), BF16), grad, grad, grad, jax.ShapeDtypeStruct((1, wide), F32)],
        scratch_shapes=scratch,
        compiler_params=pltpu.CompilerParams(
            collective_id=0, has_side_effects=True, vmem_limit_bytes=67043328),
        name="step",
    )(features, evt, w_in, w_mid, w_out, spread, bit)
    return (loss[0], gx, gi, gm, go)


def solution(mesh):
    placed = (
        P(("strata", "chain"), None),
        P(("strata", "chain"), None),
        P(("strata", "chain")),
        P(("strata", "chain")),
        P(),
        P(),
        P(),
    )
    return jax.shard_map(
        on_device,
        mesh=mesh,
        in_specs=placed,
        out_specs=(P(), P(("strata", "chain"), None), P(), P(), P()),
        check_vma=False,
    )
```

time: 565 us -> 176 us (0.31); the launches traced: 558 us -> 175 us
  waiting for transfers between devices: 237 us -> 0 us
  Pallas kernels: 0 us -> 165 us
  blocking collectives: 118 us -> 0 us
  other arithmetic: 88.2 us -> 2.5 us
  local copies, waits for them, and re-layouts: 67 us -> 7.44 us
  matrix products: 27.6 us -> 0 us
  between operations: 14.6 us -> 0.66 us
    pallas_call x0 -> x1, Pallas kernels: none -> 165 us  [on_device(): pl.pallas_call(functools.partial(step_kernel, words=words, total_rows=n *...]
    ppermute x2 -> x0, waiting for transfers between devices: 153 us -> none  [from_behind(): return lax.ppermute(block, axis, route)]
    psum x1 -> x0, waiting for transfers between devices: 83.6 us -> none  [on_device(): lax.psum((grad_in, grad_mid, grad_out, loss_part), ('strata', 'chain'))]
    psum x1 -> x0, blocking collectives: 80 us -> none  [on_device(): lax.psum((grad_in, grad_mid, grad_out, loss_part), ('strata', 'chain'))]
    all_gather x2 -> x0, blocking collectives: 37.5 us -> none  [entering(): everything = lax.all_gather(x, axis)]
    scatter-add x2 -> x0, other arithmetic: 34.8 us -> none  [the longest x1 17.5 us: on_device(): landed = jax.ops.segment_sum(weight, target, num_segments=window)]
    dot_general x9 -> x0, matrix products: 27.6 us -> none  [the longest x1 4.83 us: on_device(): preact = jnp.dot(features, w_in, preferred_element_type=jnp.float32)]
    gather x2 -> x0, local copies, waits for them, and re-layouts: 24.6 us -> none  [the longest x1 12.9 us: on_device(): exposure = before + inclusive - jnp.take(stacked, target, axis=0)]
  transfers between devices with their start and end apart: 3 -> 0, of which waited for: 3 -> 0; matrix products, arithmetic and copies ran while one was open for 4% -> 0% of each run, Pallas kernels for 0% -> 0%
where the time goes in v1:
time: 176 us; the launch traced here: 175 us
  Pallas kernels  165 us (94%)
  local copies, waits for them, and re-layouts  7.44 us (4%)
  other arithmetic  2.5 us (1%)
    pallas_call x1, Pallas kernels, on_device(): pl.pallas_call(functools.partial(step_kernel, words=words, total_rows=n *...  165 us
    unnamed x11, local copies, waits for them, and re-layouts  7.36 us

profile of v1, /device:TPU:1, one launch (start us, length us, event | category | flops | bytes accessed | tf_op | source)
XLA Modules:
  0.0 175.3 jit_solution(18066529091359689967)
XLA Ops:
  0.6 0.1 pad.3.clone
  0.7 0.7 subtract_add_fusion
  1.4 1.8 %add_add_fusion.evt = s32[40,2048]{1,0:T(8,128)} fusion(s32[1,2048]{1,0:T(1,128)S(1)} %bitcast.5, s32[1,2048]{1,0:T(1,128)S(1)} %bitcast.6, s32[35,2048]{1,0:T(8,128)} %bitcast.4, s32[40]{0:T(128)S(1)} %pad.3.clone), kind=kLoop, calls=%fused_computation | loop fusion | flops 245760 | bytes 630944 | tf_op jit(solution)/shard_map/concatenate | solution.py:422
  3.2 164.7 %step.1 = (bf16[2048,512]{1,0:T(8,128)(2,1)}, f32[512,512]{1,0:T(8,128)}, f32[512,512]{1,0:T(8,128)}, f32[512,512]{1,0:T(8,128)}, f32[1,512]{1,0:T(1,128)}) custom-call(bf16[2048,512]{1,0:T(8,128)(2,1)} %x.1, s32[40,2048]{1,0:T(8,128)} %add_add_fusion.evt, bf16[512,512]{1,0:T(8,128)(2,1)} %w_in.1, bf16[512,512]{1,0:T(8,128)(2,1)} %w_mid.1, ...), custom_call_target="tpu_custom_call" | custom-call | tf_op jit(solution)/shard_map/step/pallas_call | solution.py:448
  167.9 1.2 copy.19
  169.2 0.0 copy-start.2
  169.2 0.0 copy-start.1
  169.2 3.2 %copy.20 = bf16[2048,512]{1,0:T(8,128)(2,1)} copy(bf16[2048,512]{1,0:T(8,128)(2,1)} %get-tuple-element.23) | data formatting | bytes 4194304
  172.4 0.0 copy-done.2
  172.4 0.0 copy-start
  172.4 1.0 copy.21
  173.3 0.0 copy-done.1
  173.4 1.0 copy.22
  174.3 0.0 copy-done
  174.3 1.0 copy.23
  (1 shorter events, 0.0 us)
Async XLA Ops:
  169.2 3.2 %copy-start.2 = (f32[512,512]{1,0:T(8,128)S(1)}, f32[512,512]{1,0:T(8,128)}, u32[]{:S(2)}) copy-start(f32[512,512]{1,0:T(8,128)} %get-tuple-element.24) | copy-start | bytes 3145732
  169.2 4.2 %copy-start.1 = (f32[512,512]{1,0:T(8,128)S(1)}, f32[512,512]{1,0:T(8,128)}, u32[]{:S(2)}) copy-start(f32[512,512]{1,0:T(8,128)} %get-tuple-element.25) | copy-start | bytes 3145732
  172.4 1.9 %copy-start = (f32[512,512]{1,0:T(8,128)S(1)}, f32[512,512]{1,0:T(8,128)}, u32[]{:S(2)}) copy-start(f32[512,512]{1,0:T(8,128)} %get-tuple-element.26) | copy-start | bytes 3145732

commit v2 on v1

v2 whole, which is shorter than its diff:
```python
import functools

import jax
import jax.numpy as jnp
import numpy as np
from jax import lax
from jax.experimental import pallas as pl
from jax.experimental.pallas import tpu as pltpu
from jax.sharding import PartitionSpec as P

T = 256
Q = 512
WORD_BITS = 15
F32 = jnp.float32
BF16 = jnp.bfloat16
I32 = jnp.int32
MESH = pl.DeviceIdType.MESH


def sigmoid(v):
    return 0.5 * jnp.tanh(0.5 * v) + 0.5


def span(i, size):
    return pl.ds(pl.multiple_of(i * size, size), size)


def dot(a, b, contract=((1,), (0,))):
    return lax.dot_general(a, b, (contract, ((), ())), preferred_element_type=F32)


def mask(build):
    return jnp.concatenate([jnp.where(build(h), 1.0, 0.0).astype(BF16) for h in range(Q // 128)], axis=1)


def unpack(words, table):
    hi = lax.shift_right_logical(words, 8).astype(F32).astype(BF16)
    lo = jnp.bitwise_and(words, 255).astype(F32).astype(BF16)
    value = dot(hi, table, ((0,), (0,))) * 256.0 + dot(lo, table, ((0,), (0,)))
    return value.astype(I32)


def coordinates():
    s, c = lax.axis_index("strata"), lax.axis_index("chain")
    return {"y": s // 2, "core": s % 2, "z": c // 4, "x": c % 4}


def device(at, **moved):
    at = {**at, **moved}
    return (at["y"] * 2 + at["core"], at["z"] * 4 + at["x"])


class Reducer:
    def __init__(self, at, factor, given, outs, acc, pair, one, red, two, three, send, recv):
        self.at, self.factor, self.given, self.outs = at, factor, given, outs
        self.acc, self.pair, self.one, self.red, self.two, self.three = acc, pair, one, red, two, three
        self.send, self.recv = send, recv
        self.count, self.flying, self.copies = 0, [], {}
        self.half = acc.shape[1]
        self.stages = [self.cores, self.first, self.second, self.third, self.back_second, self.back_first,
                       self.back_cores, self.finish]

    def put(self, source, target, **moved):
        k, self.count = self.count, self.count + 1
        copy = pltpu.make_async_remote_copy(
            src_ref=source, dst_ref=target, send_sem=self.send.at[k], recv_sem=self.recv.at[k],
            device_id=device(self.at, **moved), device_id_type=MESH,
        )
        copy.start()
        self.flying.append(copy)
        return copy

    def axis(self, t, k):
        name = "xyz"[(t + k) % 3]
        return name, self.at[name]

    def others(self, name):
        return [(self.at[name] + d) % 4 for d in range(1, 4)]

    def arrived(self, t):
        for copy in self.copies[t]:
            copy.wait_recv()

    def stage(self, k, t):
        self.stages[k](t)

    def cores(self, t):
        core = self.at["core"]
        away = span(1 - core, self.half)
        self.copies[t] = [self.put(self.given[t].at[away], self.pair.at[t], core=1 - core)]

    def first(self, t):
        name, p = self.axis(t, 0)
        self.arrived(t)
        self.acc[t] = (self.given[t][span(self.at["core"], self.half), :] + self.pair[t]) * self.factor
        size = self.half // 4
        self.copies[t] = [
            self.put(self.acc.at[t, span(to, size)], self.one.at[t, p], **{name: to}) for to in self.others(name)
        ]

    def second(self, t):
        name, p = self.axis(t, 0)
        self.arrived(t)
        total = self.acc[t, span(p, self.half // 4), :]
        for other in self.others(name):
            total = total + self.one[t, other]
        self.red[t] = total
        name, q = self.axis(t, 1)
        size = self.half // 16
        self.copies[t] = [
            self.put(self.red.at[t, span(to, size)], self.two.at[t, q], **{name: to}) for to in self.others(name)
        ]

    def third(self, t):
        name, q = self.axis(t, 1)
        self.arrived(t)
        total = self.red[t, span(q, self.half // 16), :]
        for other in self.others(name):
            total = total + self.two[t, other]
        name, r = self.axis(t, 2)
        self.three[t, r] = total
        self.copies[t] = [
            self.put(self.three.at[t, r], self.three.at[t, r], **{name: to}) for to in self.others(name)
        ]

    def rows(self, t, fine):
        p, q = self.axis(t, 0)[1], self.axis(t, 1)[1]
        block = self.at["core"] * 4 + p
        return span(block * 4 + q, self.half // 16) if fine else span(block, self.half // 4)

    def back_second(self, t):
        self.arrived(t)
        rows = self.rows(t, True)
        self.outs[t][rows, :] = self.three[t, 0] + self.three[t, 1] + self.three[t, 2] + self.three[t, 3]
        name = self.axis(t, 1)[0]
        self.copies[t] = [
            self.put(self.outs[t].at[rows], self.outs[t].at[rows], **{name: to}) for to in self.others(name)
        ]

    def back_first(self, t):
        self.arrived(t)
        rows = self.rows(t, False)
        name = self.axis(t, 0)[0]
        self.copies[t] = [
            self.put(self.outs[t].at[rows], self.outs[t].at[rows], **{name: to}) for to in self.others(name)
        ]
        self.own = getattr(self, "own", {})
        self.own[t] = self.put(self.outs[t].at[rows], self.outs[t].at[rows], core=1 - self.at["core"])

    def back_cores(self, t):
        name, p = self.axis(t, 0)
        later = [self.own[t]]
        for d, copy in enumerate(self.copies[t]):
            copy.wait_recv()
            rows = span(self.at["core"] * 4 + (p + 3 - d) % 4, self.half // 4)
            later.append(self.put(self.outs[t].at[rows], self.outs[t].at[rows], core=1 - self.at["core"]))
        self.copies[t] = later

    def finish(self, t):
        self.arrived(t)

    def drain(self):
        for copy in self.flying:
            copy.wait_send()


class Tally:
    def __init__(self, reducer, ref):
        self.reducer, self.ref, self.copies = reducer, ref, None

    def send(self, k, value):
        axis = ("core", "x", "y", "z")[k]
        at, n = self.reducer.at, 2 if k == 0 else 4
        slot = self.ref.at[k, at[axis]]
        self.ref[k, at[axis]] = value
        self.copies = [self.reducer.put(slot, slot, **{axis: (at[axis] + d) % n}) for d in range(1, n)]

    def total(self, k):
        for copy in self.copies:
            copy.wait_recv()
        total = self.ref[k, 0]
        for slot in range(1, 2 if k == 0 else 4):
            total = total + self.ref[k, slot]
        return total


def step_kernel(
    x_in, w_in_in, w_mid_in, w_out_in, events, tie, entry_in, spread, bit,
    gx_out, go_out, gm_out, gi_out, loss_out,
    x, w_in, w_mid, w_out, x_t, fh_t, hid_t, s1, s2, ind, indp, wb, w, wn, wp, own, prev, hb, hp, nb, pb,
    first_col, firstp_col, entry_col, evt, evp, idxn, logs, g, acc, pair, one, red, two, three, tally,
    in_sem, small_send, small_recv, w_send, w_recv, gx_sem, send, recv, *, words, total_rows, chain,
):
    n, wide = x.shape[0], w_out.shape[1]
    parts, part = w.shape[0], w.shape[2]
    tiles, quarters = n // T, n // Q
    at = coordinates()
    me = lax.axis_index("chain")
    strata = lax.axis_index("strata")
    right, left = (strata, (me + 1) % chain), (strata, (me + chain - 1) % chain)

    barrier = pltpu.get_barrier_semaphore()
    friends = [left, right, device(at, core=1 - at["core"])]
    for axis in "xyz":
        friends += [device(at, **{axis: (at[axis] + d) % 4}) for d in range(1, 4)]
    for friend in friends:
        pl.semaphore_signal(barrier, inc=1, device_id=friend, device_id_type=MESH)
    loads = [
        pltpu.make_async_copy(source, target, in_sem.at[k])
        for k, (source, target) in enumerate(((x_in, x), (w_in_in, w_in), (w_mid_in, w_mid), (w_out_in, w_out)))
    ]
    for load in loads:
        load.start()
    evt[0:words, :] = events[...]
    evt[words : words + 1, :] = tie[...] - me * n
    evt[words + 1 : words + 2, :] = entry_in[...] - me * n + n
    evt[words + 2 :, :] = jnp.zeros((evt.shape[0] - words - 2, n), I32)
    pl.semaphore_wait(barrier, len(friends))

    def remote(source, target, s, r, to):
        return pltpu.make_async_remote_copy(
            src_ref=source, dst_ref=target, send_sem=s, recv_sem=r, device_id=to, device_id_type=MESH)

    top = words // 8 * 8
    ev_copy = remote(evt, evp, small_send.at[0], small_recv.at[0], right)
    id_copy = remote(evt.at[pl.ds(top, 8)], idxn, small_send.at[1], small_recv.at[1], left)
    ev_copy.start()
    id_copy.start()

    def to_left(c, r):
        rows = span(r, T)
        return remote(w.at[c, rows], wn.at[c, rows], w_send.at[0, c, r], w_recv.at[0, c, r], left)

    def to_right(c, r):
        rows = span(r, T)
        return remote(w.at[c, rows], wp.at[c, rows], w_send.at[1, c, r], w_recv.at[1, c, r], right)

    logs[...] = jnp.zeros_like(logs)
    for load in loads:
        load.wait()

    def forward(r, _):
        rows = span(r, T)
        pre = dot(x[rows, :], w_in[...])
        s = sigmoid(pre)
        first = (pre * s).astype(BF16)
        s1[rows, :] = (s * (1.0 + pre * (1.0 - s))).astype(BF16)
        mid = dot(first, w_mid[...])
        s = sigmoid(mid)
        hidden = (mid * s).astype(BF16)
        s2[rows, :] = (s * (1.0 + mid * (1.0 - s))).astype(BF16)
        eta = dot(hidden, w_out[...])
        weight = jnp.exp(eta)
        for c in range(parts):
            w[c, rows, :] = weight[:, c * part : (c + 1) * part]
        to_left(0, r).start()
        to_right(0, r).start()
        wb[rows, :] = weight.astype(BF16)
        fh_t[:, rows] = first.T
        hid_t[:, rows] = hidden.T
        value = unpack(evt[:, rows], spread[...])
        flag = jnp.bitwise_and(lax.shift_right_logical(value[:, :wide], bit[...]), 1).astype(F32)
        ind[rows, :] = flag.astype(BF16)
        first_col[rows, :] = value[:, wide : wide + 128]
        entry_col[rows, :] = value[:, wide + 128 : wide + 256]
        logs[...] -= jnp.sum((flag * eta).reshape(-1, 8, wide), axis=0)
        return 0

    lax.fori_loop(0, tiles, forward, 0)

    def later(r, _):
        for c in range(1, parts):
            to_left(c, r).start()
            to_right(c, r).start()
        return 0

    lax.fori_loop(0, tiles, later, 0)

    ev_copy.wait_recv()
    id_copy.wait_recv()
    real = jnp.where(me > 0, 1.0, 0.0).astype(F32)
    idxn[...] = idxn[...] + jnp.where(me == chain - 1, 1 << 20, 0)

    def unpack_prev(r, _):
        rows = span(r, T)
        value = unpack(evp[:, rows], spread[...])
        flag = jnp.bitwise_and(lax.shift_right_logical(value[:, :wide], bit[...]), 1).astype(F32)
        indp[rows, :] = (flag * real).astype(BF16)
        firstp_col[rows, :] = value[:, wide : wide + 128]
        x_t[:, rows] = x[rows, :].T
        return 0

    lax.fori_loop(0, tiles, unpack_prev, 0)

    def lane(base):
        return lax.broadcasted_iota(I32, (Q, 128), 1) + base

    def row(table, k, j, h):
        return table[k : k + 1, j * Q + h * 128 : j * Q + (h + 1) * 128]

    FIRST, ENTRY, ENTRY_N = words, words + 1, words + 1 - top

    def own_part(i, _):
        rows = span(i, Q)
        first, firstp = first_col[rows, :], firstp_col[rows, :]
        total = totalp = 0.0
        for j in range(quarters):
            m = mask(lambda h: (row(evt, ENTRY, j, h) <= first + n) & (first <= lane(j * Q + h * 128)))
            total += dot(m, wb[j * Q : (j + 1) * Q, :])
        for c in range(parts):
            own[c, rows, :] = total[:, c * part : (c + 1) * part]
        for j in range(quarters):
            m = mask(lambda h: row(evt, ENTRY, j, h) <= firstp)
            totalp += dot(m, wb[j * Q : (j + 1) * Q, :])
        for c in range(parts):
            prev[c, rows, :] = totalp[:, c * part : (c + 1) * part]
        return 0

    lax.fori_loop(0, quarters, own_part, 0)

    def add_logs(c):
        cols = slice(c * part, (c + 1) * part)

        def tile(i, _):
            rows = span(i, T)
            log = jnp.where(ind[rows, cols].astype(F32) > 0.0, jnp.log(own[c, rows, :]), 0.0)
            logs[:, cols] += jnp.sum(log.reshape(-1, 8, part), axis=0)
            return 0

        lax.fori_loop(0, tiles, tile, 0)

    eta_ref = wb
    for c in range(parts):
        cols = slice(c * part, (c + 1) * part)
        for q in range(quarters):
            for r in range(q * Q // T, (q + 1) * Q // T):
                to_left(c, r).wait_recv()
                to_right(c, r).wait_recv()
            nb[...] = wn[c, q * Q : (q + 1) * Q, :].astype(BF16)
            pb[...] = wp[c, q * Q : (q + 1) * Q, :].astype(BF16)

            def arrive(i, _):
                rows = span(i, Q)
                first, firstp = first_col[rows, :], firstp_col[rows, :]
                own[c, rows, :] += dot(mask(lambda h: row(idxn, ENTRY_N, q, h) <= first), nb[...])
                m = mask(lambda h: (row(evp, ENTRY, q, h) <= firstp + n) & (firstp <= lane(q * Q + h * 128)))
                prev[c, rows, :] += dot(m, pb[...])
                return 0

            lax.fori_loop(0, quarters, arrive, 0)

        def hazards(i, _):
            rows = span(i, T)
            divisor = own[c, rows, :]
            flag = ind[rows, cols].astype(F32) > 0.0
            hb[rows, :] = jnp.where(flag, 1.0 / divisor, 0.0).astype(BF16)
            flagp = indp[rows, cols].astype(F32) > 0.0
            hp[rows, :] = jnp.where(flagp, 1.0 / prev[c, rows, :], 0.0).astype(BF16)
            return 0

        lax.fori_loop(0, tiles, hazards, 0)

        def expose(j, _):
            rows = span(j, Q)
            entry = entry_col[rows, :]
            here = lax.broadcasted_iota(I32, (Q, 128), 0) + j * Q
            total = 0.0
            for i in range(quarters):
                block = slice(i * Q, (i + 1) * Q)
                m = mask(lambda h: (entry <= row(evt, FIRST, i, h) + n) & (row(evt, FIRST, i, h) <= here))
                total += dot(m, hb[block, :])
                total += dot(mask(lambda h: entry <= row(evp, FIRST, i, h)), hp[block, :])
            eta_ref[rows, cols] = (w[c, rows, :] * total - ind[rows, cols].astype(F32)).astype(BF16)
            return 0

        lax.fori_loop(0, quarters, expose, 0)
        g[0, :, cols] = dot(hid_t[...], eta_ref[:, cols])
        if c < parts - 1:
            add_logs(c)

    mid_ref, pre_ref, gx = s2, s1, x
    reducer = Reducer(at, total_rows ** (-0.5), [g.at[t] for t in range(3)], [go_out, gm_out, gi_out],
                      acc, pair, one, red, two, three, send, recv)
    counted = Tally(reducer, tally)

    def turn(k):
        for t in range(2, -1, -1):
            if 0 <= k - t < len(reducer.stages):
                reducer.stage(k - t, t)

    turn(0)

    def middle(i, _):
        rows = span(i, Q)
        mid_grad = dot(eta_ref[rows, :], w_out[...], ((1,), (1,))) * s2[rows, :].astype(F32)
        mid_ref[rows, :] = mid_grad.astype(BF16)
        return 0

    lax.fori_loop(0, quarters, middle, 0)
    g[1] = dot(fh_t[...], mid_ref[...])
    turn(1)

    def inner(i, _):
        rows = span(i, Q)
        pre_grad = dot(mid_ref[rows, :], w_mid[...], ((1,), (1,))) * s1[rows, :].astype(F32)
        pre_ref[rows, :] = pre_grad.astype(BF16)
        return 0

    lax.fori_loop(0, quarters, inner, 0)
    g[2] = dot(x_t[...], pre_ref[...])
    turn(2)
    add_logs(parts - 1)
    counted.send(0, logs[...] / total_rows)

    def last(i, _):
        rows = span(i, Q)
        gx[rows, :] = dot(pre_ref[rows, :], w_in[...], ((1,), (1,))).astype(BF16)
        return 0

    turn(3)
    counted.send(1, counted.total(0))
    lax.fori_loop(0, quarters, last, 0)
    gx_copy = pltpu.make_async_copy(gx, gx_out, gx_sem)
    gx_copy.start()
    turn(4)
    counted.send(2, counted.total(1))
    turn(5)
    counted.send(3, counted.total(2))
    turn(6)
    loss_out[...] = jnp.sum(counted.total(3), axis=0, keepdims=True)
    for k in range(7, len(reducer.stages) + 2):
        turn(k)
    reducer.drain()
    gx_copy.wait()
    ev_copy.wait_send()
    id_copy.wait_send()

    def drain(r, _):
        for c in range(parts):
            to_left(c, r).wait_send()
            to_right(c, r).wait_send()
        return 0

    lax.fori_loop(0, tiles, drain, 0)


def copy_kernel(*refs):
    m = len(refs) // 2
    for source, target in zip(refs[:m], refs[m:]):
        target[...] = source[...]


def on_device(features, events, tie_first, entry_row, w_in, w_mid, w_out):
    n, width = features.shape
    hidden_width, wide = w_out.shape
    words = events.shape[1]
    chain, strata = lax.axis_size("chain"), lax.axis_size("strata")
    assert (width, hidden_width, wide, n % Q) == (512, 512, 512, 0) and words % 8 in range(1, 7)
    parts = 2
    part = wide // parts
    deep = words // 8 * 8 + 8
    column = np.arange(wide + 256)
    source = np.where(column < wide, column // WORD_BITS, words + (column - wide) // 128)
    spread = jnp.asarray((source[None, :] == np.arange(deep)[:, None]).astype(np.float32), BF16)
    bit = jnp.asarray((np.arange(wide) % WORD_BITS)[None, :].astype(np.int32))

    m = 3
    half = hidden_width // 2
    messages = m * 20 + 10
    V = pltpu.VMEM
    dma = pltpu.SemaphoreType.DMA
    by_rows, by_columns, square = V((n, wide), BF16), V((wide, n), BF16), V((wide, wide), BF16)
    scratch = (
        [by_rows] + [square] * 3 + [by_columns] * 3 + [by_rows] * 5
        + [V((parts, n, part), F32)] * 5
        + [V((n, part), BF16)] * 2 + [V((Q, part), BF16)] * 2 + [V((n, 128), I32)] * 3
        + [V((deep, n), I32)] * 2 + [V((8, n), I32), V((8, wide), F32), V((m, hidden_width, wide), F32)]
        + [V((m, half, wide), F32)] * 2
        + [V((m, 4, half // 4, wide), F32), V((m, half // 4, wide), F32)]
        + [V((m, 4, half // 16, wide), F32)] * 2 + [V((4, 4, 8, wide), F32)]
        + [dma((4,))] + [dma((2,))] * 2 + [dma((2, parts, n // T))] * 2 + [dma, dma((messages,)), dma((messages,))]
    )
    vmem = pl.BlockSpec(memory_space=V)
    anywhere = pl.BlockSpec(memory_space=pl.ANY)
    grad = jax.ShapeDtypeStruct((hidden_width, wide), F32)
    shapes = [jax.ShapeDtypeStruct((n, width), BF16), grad, grad, grad, jax.ShapeDtypeStruct((1, wide), F32)]
    results = pl.pallas_call(
        functools.partial(step_kernel, words=words, total_rows=n * chain * strata, chain=chain),
        in_specs=[anywhere] * 4 + [vmem] * 5,
        out_specs=[anywhere] + [vmem] * 4,
        out_shape=shapes,
        scratch_shapes=scratch,
        compiler_params=pltpu.CompilerParams(
            collective_id=0, has_side_effects=True, vmem_limit_bytes=67043328),
        name="step",
    )(features, w_in, w_mid, w_out, events.T, tie_first[None], entry_row[None], spread, bit)
    steps = 4
    blocks = [pl.BlockSpec((r.shape[0] // steps, r.shape[1]), lambda i: (i, 0)) for r in shapes[:4]]
    blocks.append(pl.BlockSpec(shapes[4].shape, lambda i: (0, 0)))
    gx, go, gm, gi, loss = pl.pallas_call(
        copy_kernel, grid=(steps,), in_specs=blocks, out_specs=blocks, out_shape=shapes, name="results",
    )(*results)
    return (loss[0], gx, gi, gm, go)


def solution(mesh):
    placed = (
        P(("strata", "chain"), None),
        P(("strata", "chain"), None),
        P(("strata", "chain")),
        P(("strata", "chain")),
        P(),
        P(),
        P(),
    )
    return jax.shard_map(
        on_device,
        mesh=mesh,
        in_specs=placed,
        out_specs=(P(), P(("strata", "chain"), None), P(), P(), P()),
        check_vma=False,
    )
```

time: 176 us -> 167 us (0.949)
  local copies, waits for them, and re-layouts: 7.44 us -> 0 us
  other arithmetic: 2.5 us -> 0 us
    unnamed x11 -> x0, local copies, waits for them, and re-layouts: 7.36 us -> none
    pallas_call x0 -> x1, Pallas kernels: none -> 5.27 us  [on_device(): pl.pallas_call(copy_kernel, grid=(steps,), in_specs=blocks, out_specs=blo...]
    pallas_call x1, Pallas kernels: 165 us -> 161 us  [on_device(): pl.pallas_call(functools.partial(step_kernel, words=words, total_rows=n *...]
    concatenate x1 -> x0, other arithmetic: 1.79 us -> none  [on_device(): jnp.concatenate([events.T, (tie_first - start)[None], (entry_row - start...]
where the time goes in v2:
time: 167 us
  Pallas kernels  166 us (99%)
    pallas_call x1, Pallas kernels, on_device(): pl.pallas_call(functools.partial(step_kernel, words=words, total_rows=n *...  161 us
    pallas_call x1, Pallas kernels, on_device(): pl.pallas_call(copy_kernel, grid=(steps,), in_specs=blocks, out_specs=blo...  5.27 us

profile of v2, /device:TPU:1, one launch (start us, length us, event | category | flops | bytes accessed | tf_op | source)
XLA Modules:
  0.0 166.8 jit_solution(3578386647979170632)
XLA Ops:
  0.6 160.9 %step.1 = (bf16[2048,512]{1,0:T(8,128)(2,1)}, f32[512,512]{1,0:T(8,128)}, f32[512,512]{1,0:T(8,128)}, f32[512,512]{1,0:T(8,128)}, f32[1,512]{1,0:T(1,128)}) custom-call(bf16[2048,512]{1,0:T(8,128)(2,1)} %x_in.1, bf16[512,512]{1,0:T(8,128)(2,1)} %w_in_in.1, bf16[512,512]{1,0:T(8,128)(2,1)} %w_mid_in.1, bf16[512,512]{1,0:T(8,128)(2,1)} %w_out_in.1, ...), custom_call_target="tpu_custom_call" | custom-call | tf_op jit(solution)/shard_map/step/pallas_call | solution.py:487
  161.5 5.3 %results.1 = (bf16[2048,512]{1,0:T(8,128)(2,1)}, f32[512,512]{1,0:T(8,128)}, f32[512,512]{1,0:T(8,128)}, f32[512,512]{1,0:T(8,128)}, f32[1,512]{1,0:T(1,128)}) custom-call(bf16[2048,512]{1,0:T(8,128)(2,1)} %get-tuple-element.15.refs_0_, f32[512,512]{1,0:T(8,128)} %get-tuple-element.16.refs_1_, f32[512,512]{1,0:T(8,128)} %get-tuple-element.17.refs_2_, ...), custom_call_target="tpu_custom_call" | custom-call | tf_op jit(solution)/shard_map/results/pallas_call | solution.py:500

commit v3 on v2

--- a/solution.py
+++ b/solution.py
@@ -55,8 +55,8 @@
         self.at, self.factor, self.given, self.outs = at, factor, given, outs
         self.acc, self.pair, self.one, self.red, self.two, self.three = acc, pair, one, red, two, three
         self.send, self.recv = send, recv
-        self.count, self.flying, self.copies = 0, [], {}
-        self.half = acc.shape[1]
+        self.count, self.flying, self.copies, self.own = 0, [], {}, {}
+        self.block, self.per = acc.shape[1], acc.shape[0] // len(given)
         self.stages = [self.cores, self.first, self.second, self.third, self.back_second, self.back_first,
                        self.back_cores, self.finish]
 
@@ -75,7 +75,11 @@
         return name, self.at[name]
 
     def others(self, name):
-        return [(self.at[name] + d) % 4 for d in range(1, 4)]
+        return [(self.at[name] + d) % 4 for d in (2, 1, 3)]
+
+    def rows_of(self, t, core, start, size):
+        blocks = self.block // size
+        return span((core * self.per + t % self.per) * blocks + start, size)
 
     def arrived(self, t):
         for copy in self.copies[t]:
@@ -86,14 +90,15 @@
 
     def cores(self, t):
         core = self.at["core"]
-        away = span(1 - core, self.half)
-        self.copies[t] = [self.put(self.given[t].at[away], self.pair.at[t], core=1 - core)]
+        away = self.rows_of(t, 1 - core, 0, self.block)
+        self.copies[t] = [self.put(self.given[t // self.per].at[away], self.pair.at[t], core=1 - core)]
 
     def first(self, t):
         name, p = self.axis(t, 0)
         self.arrived(t)
-        self.acc[t] = (self.given[t][span(self.at["core"], self.half), :] + self.pair[t]) * self.factor
-        size = self.half // 4
+        kept = self.rows_of(t, self.at["core"], 0, self.block)
+        self.acc[t] = (self.given[t // self.per][kept, :] + self.pair[t]) * self.factor
+        size = self.block // 4
         self.copies[t] = [
             self.put(self.acc.at[t, span(to, size)], self.one.at[t, p], **{name: to}) for to in self.others(name)
         ]
@@ -101,12 +106,12 @@
     def second(self, t):
         name, p = self.axis(t, 0)
         self.arrived(t)
-        total = self.acc[t, span(p, self.half // 4), :]
+        total = self.acc[t, span(p, self.block // 4), :]
         for other in self.others(name):
             total = total + self.one[t, other]
         self.red[t] = total
         name, q = self.axis(t, 1)
-        size = self.half // 16
+        size = self.block // 16
         self.copies[t] = [
             self.put(self.red.at[t, span(to, size)], self.two.at[t, q], **{name: to}) for to in self.others(name)
         ]
@@ -114,7 +119,7 @@
     def third(self, t):
         name, q = self.axis(t, 1)
         self.arrived(t)
-        total = self.red[t, span(q, self.half // 16), :]
+        total = self.red[t, span(q, self.block // 16), :]
         for other in self.others(name):
             total = total + self.two[t, other]
         name, r = self.axis(t, 2)
@@ -125,35 +130,35 @@
 
     def rows(self, t, fine):
         p, q = self.axis(t, 0)[1], self.axis(t, 1)[1]
-        block = self.at["core"] * 4 + p
-        return span(block * 4 + q, self.half // 16) if fine else span(block, self.half // 4)
+        core = self.at["core"]
+        return self.rows_of(t, core, p * 4 + q, self.block // 16) if fine else self.rows_of(t, core, p, self.block // 4)
+
+    def spread(self, t, rows, name):
+        piece = self.outs[t // self.per].at[rows]
+        return [self.put(piece, piece, **{name: to}) for to in self.others(name)]
 
     def back_second(self, t):
         self.arrived(t)
         rows = self.rows(t, True)
-        self.outs[t][rows, :] = self.three[t, 0] + self.three[t, 1] + self.three[t, 2] + self.three[t, 3]
-        name = self.axis(t, 1)[0]
-        self.copies[t] = [
-            self.put(self.outs[t].at[rows], self.outs[t].at[rows], **{name: to}) for to in self.others(name)
-        ]
+        total = self.three[t, 0] + self.three[t, 1] + self.three[t, 2] + self.three[t, 3]
+        self.outs[t // self.per][rows, :] = total
+        self.copies[t] = self.spread(t, rows, self.axis(t, 1)[0])
 
     def back_first(self, t):
         self.arrived(t)
         rows = self.rows(t, False)
-        name = self.axis(t, 0)[0]
-        self.copies[t] = [
-            self.put(self.outs[t].at[rows], self.outs[t].at[rows], **{name: to}) for to in self.others(name)
-        ]
-        self.own = getattr(self, "own", {})
-        self.own[t] = self.put(self.outs[t].at[rows], self.outs[t].at[rows], core=1 - self.at["core"])
+        self.copies[t] = self.spread(t, rows, self.axis(t, 0)[0])
+        piece = self.outs[t // self.per].at[rows]
+        self.own[t] = self.put(piece, piece, core=1 - self.at["core"])
 
     def back_cores(self, t):
-        name, p = self.axis(t, 0)
+        p = self.axis(t, 0)[1]
         later = [self.own[t]]
-        for d, copy in enumerate(self.copies[t]):
+        for d, copy in zip((2, 1, 3), self.copies[t]):
             copy.wait_recv()
-            rows = span(self.at["core"] * 4 + (p + 3 - d) % 4, self.half // 4)
-            later.append(self.put(self.outs[t].at[rows], self.outs[t].at[rows], core=1 - self.at["core"]))
+            rows = self.rows_of(t, self.at["core"], (p + 4 - d) % 4, self.block // 4)
+            piece = self.outs[t // self.per].at[rows]
+            later.append(self.put(piece, piece, core=1 - self.at["core"]))
         self.copies[t] = later
 
     def finish(self, t):
@@ -187,9 +192,9 @@
 def step_kernel(
     x_in, w_in_in, w_mid_in, w_out_in, events, tie, entry_in, spread, bit,
     gx_out, go_out, gm_out, gi_out, loss_out,
-    x, w_in, w_mid, w_out, x_t, fh_t, hid_t, s1, s2, ind, indp, wb, w, wn, wp, own, prev, hb, hp, nb, pb,
+    sums, x, w_in, w_mid, w_out, x_t, fh_t, hid_t, s1, s2, ind, indp, wb, w, wn, wp, own, prev, hb, hp, nb, pb,
     first_col, firstp_col, entry_col, evt, evp, idxn, logs, g, acc, pair, one, red, two, three, tally,
-    in_sem, small_send, small_recv, w_send, w_recv, gx_sem, send, recv, *, words, total_rows, chain,
+    in_sem, out_sem, small_send, small_recv, w_send, w_recv, gx_sem, send, recv, *, words, total_rows, chain,
 ):
     n, wide = x.shape[0], w_out.shape[1]
     parts, part = w.shape[0], w.shape[2]
@@ -330,46 +335,72 @@
         lax.fori_loop(0, tiles, tile, 0)
 
     eta_ref = wb
+
+    def from_next(c, q):
+        for r in range(q * Q // T, (q + 1) * Q // T):
+            to_left(c, r).wait_recv()
+        nb[...] = wn[c, q * Q : (q + 1) * Q, :].astype(BF16)
+
+        def tile(i, _):
+            rows = span(i, Q)
+            first = first_col[rows, :]
+            own[c, rows, :] += dot(mask(lambda h: row(idxn, ENTRY_N, q, h) <= first), nb[...])
+            return 0
+
+        lax.fori_loop(0, quarters, tile, 0)
+
+    def from_previous(c, q):
+        for r in range(q * Q // T, (q + 1) * Q // T):
+            to_right(c, r).wait_recv()
+        pb[...] = wp[c, q * Q : (q + 1) * Q, :].astype(BF16)
+
+        def tile(i, _):
+            rows = span(i, Q)
+            firstp = firstp_col[rows, :]
+            m = mask(lambda h: (row(evp, ENTRY, q, h) <= firstp + n) & (firstp <= lane(q * Q + h * 128)))
+            prev[c, rows, :] += dot(m, pb[...])
+            return 0
+
+        lax.fori_loop(0, quarters, tile, 0)
+
+    def hazards(flags, divisors, target):
+        def tile(i, _):
+            rows = span(i, T)
+            flag = flags(rows).astype(F32) > 0.0
+            target[rows, :] = jnp.where(flag, 1.0 / divisors(rows), 0.0).astype(BF16)
+            return 0
+
+        lax.fori_loop(0, tiles, tile, 0)
+
     for c in range(parts):
         cols = slice(c * part, (c + 1) * part)
         for q in range(quarters):
-            for r in range(q * Q // T, (q + 1) * Q // T):
-                to_left(c, r).wait_recv()
-                to_right(c, r).wait_recv()
-            nb[...] = wn[c, q * Q : (q + 1) * Q, :].astype(BF16)
-            pb[...] = wp[c, q * Q : (q + 1) * Q, :].astype(BF16)
-
-            def arrive(i, _):
-                rows = span(i, Q)
-                first, firstp = first_col[rows, :], firstp_col[rows, :]
-                own[c, rows, :] += dot(mask(lambda h: row(idxn, ENTRY_N, q, h) <= first), nb[...])
-                m = mask(lambda h: (row(evp, ENTRY, q, h) <= firstp + n) & (firstp <= lane(q * Q + h * 128)))
-                prev[c, rows, :] += dot(m, pb[...])
-                return 0
-
-            lax.fori_loop(0, quarters, arrive, 0)
-
-        def hazards(i, _):
-            rows = span(i, T)
-            divisor = own[c, rows, :]
-            flag = ind[rows, cols].astype(F32) > 0.0
-            hb[rows, :] = jnp.where(flag, 1.0 / divisor, 0.0).astype(BF16)
-            flagp = indp[rows, cols].astype(F32) > 0.0
-            hp[rows, :] = jnp.where(flagp, 1.0 / prev[c, rows, :], 0.0).astype(BF16)
-            return 0
-
-        lax.fori_loop(0, tiles, hazards, 0)
-
-        def expose(j, _):
+            from_next(c, q)
+            if q < quarters - 1:
+                from_previous(c, q)
+        hazards(lambda rows: ind[rows, cols], lambda rows: own[c, rows, :], hb)
+
+        def expose_own(j, _):
             rows = span(j, Q)
             entry = entry_col[rows, :]
             here = lax.broadcasted_iota(I32, (Q, 128), 0) + j * Q
             total = 0.0
             for i in range(quarters):
-                block = slice(i * Q, (i + 1) * Q)
                 m = mask(lambda h: (entry <= row(evt, FIRST, i, h) + n) & (row(evt, FIRST, i, h) <= here))
-                total += dot(m, hb[block, :])
-                total += dot(mask(lambda h: entry <= row(evp, FIRST, i, h)), hp[block, :])
+                total += dot(m, hb[i * Q : (i + 1) * Q, :])
+            wn[c, rows, :] = total
+            return 0
+
+        lax.fori_loop(0, quarters, expose_own, 0)
+        from_previous(c, quarters - 1)
+        hazards(lambda rows: indp[rows, cols], lambda rows: prev[c, rows, :], hp)
+
+        def expose(j, _):
+            rows = span(j, Q)
+            entry = entry_col[rows, :]
+            total = wn[c, rows, :]
+            for i in range(quarters):
+                total += dot(mask(lambda h: entry <= row(evp, FIRST, i, h)), hp[i * Q : (i + 1) * Q, :])
             eta_ref[rows, cols] = (w[c, rows, :] * total - ind[rows, cols].astype(F32)).astype(BF16)
             return 0
 
@@ -379,14 +410,19 @@
             add_logs(c)
 
     mid_ref, pre_ref, gx = s2, s1, x
-    reducer = Reducer(at, total_rows ** (-0.5), [g.at[t] for t in range(3)], [go_out, gm_out, gi_out],
+    reducer = Reducer(at, total_rows ** (-0.5), [g.at[t] for t in range(3)], [sums.at[t] for t in range(3)],
                       acc, pair, one, red, two, three, send, recv)
     counted = Tally(reducer, tally)
+
+    outs = [pltpu.make_async_copy(sums.at[t], out, out_sem.at[t]) for t, out in enumerate((go_out, gm_out, gi_out))]
 
     def turn(k):
         for t in range(2, -1, -1):
             if 0 <= k - t < len(reducer.stages):
-                reducer.stage(k - t, t)
+                for v in range(reducer.per):
+                    reducer.stage(k - t, t * reducer.per + v)
+                if k - t == len(reducer.stages) - 1:
+                    outs[t].start()
 
     turn(0)
 
@@ -432,6 +468,8 @@
         turn(k)
     reducer.drain()
     gx_copy.wait()
+    for out in outs:
+        out.wait()
     ev_copy.wait_send()
     id_copy.wait_send()
 
@@ -445,9 +483,24 @@
 
 
 def copy_kernel(*refs):
-    m = len(refs) // 2
-    for source, target in zip(refs[:m], refs[m:]):
-        target[...] = source[...]
+    m = (len(refs) - 2) // 3
+    sources, targets, buffers, sem_in, sem_out = refs[:m], refs[m : 2 * m], refs[2 * m : 3 * m], refs[-2], refs[-1]
+    reads, writes = [], []
+    for source, target, buffer in zip(sources, targets, buffers):
+        pieces = max(source.shape[0] // 256, 1) if source.dtype == F32 else source.shape[0] // 512
+        size = source.shape[0] // pieces
+        for k in range(pieces):
+            at = pl.ds(k * size, size)
+            i = len(reads)
+            reads.append(pltpu.make_async_copy(source.at[at], buffer.at[at], sem_in.at[i]))
+            writes.append(pltpu.make_async_copy(buffer.at[at], target.at[at], sem_out.at[i]))
+    for read in reads:
+        read.start()
+    for read, write in zip(reads, writes):
+        read.wait()
+        write.start()
+    for write in writes:
+        write.wait()
 
 
 def on_device(features, events, tie_first, entry_row, w_in, w_mid, w_out):
@@ -465,20 +518,21 @@
     bit = jnp.asarray((np.arange(wide) % WORD_BITS)[None, :].astype(np.int32))
 
     m = 3
-    half = hidden_width // 2
-    messages = m * 20 + 10
+    per = 2
+    streams, block = m * per, hidden_width // 2 // per
+    messages = streams * 20 + 10
     V = pltpu.VMEM
     dma = pltpu.SemaphoreType.DMA
     by_rows, by_columns, square = V((n, wide), BF16), V((wide, n), BF16), V((wide, wide), BF16)
     scratch = (
-        [by_rows] + [square] * 3 + [by_columns] * 3 + [by_rows] * 5
+        [V((m, hidden_width, wide), F32), by_rows] + [square] * 3 + [by_columns] * 3 + [by_rows] * 5
         + [V((parts, n, part), F32)] * 5
         + [V((n, part), BF16)] * 2 + [V((Q, part), BF16)] * 2 + [V((n, 128), I32)] * 3
         + [V((deep, n), I32)] * 2 + [V((8, n), I32), V((8, wide), F32), V((m, hidden_width, wide), F32)]
-        + [V((m, half, wide), F32)] * 2
-        + [V((m, 4, half // 4, wide), F32), V((m, half // 4, wide), F32)]
-        + [V((m, 4, half // 16, wide), F32)] * 2 + [V((4, 4, 8, wide), F32)]
-        + [dma((4,))] + [dma((2,))] * 2 + [dma((2, parts, n // T))] * 2 + [dma, dma((messages,)), dma((messages,))]
+        + [V((streams, block, wide), F32)] * 2
+        + [V((streams, 4, block // 4, wide), F32), V((streams, block // 4, wide), F32)]
+        + [V((streams, 4, block // 16, wide), F32)] * 2 + [V((4, 4, 8, wide), F32)]
+        + [dma((4,)), dma((m,))] + [dma((2,))] * 2 + [dma((2, parts, n // T))] * 2 + [dma, dma((messages,)), dma((messages,))]
     )
     vmem = pl.BlockSpec(memory_space=V)
     anywhere = pl.BlockSpec(memory_space=pl.ANY)
@@ -487,18 +541,20 @@
     results = pl.pallas_call(
         functools.partial(step_kernel, words=words, total_rows=n * chain * strata, chain=chain),
         in_specs=[anywhere] * 4 + [vmem] * 5,
-        out_specs=[anywhere] + [vmem] * 4,
+        out_specs=[anywhere] * 4 + [vmem],
         out_shape=shapes,
         scratch_shapes=scratch,
         compiler_params=pltpu.CompilerParams(
             collective_id=0, has_side_effects=True, vmem_limit_bytes=67043328),
         name="step",
     )(features, w_in, w_mid, w_out, events.T, tie_first[None], entry_row[None], spread, bit)
-    steps = 4
-    blocks = [pl.BlockSpec((r.shape[0] // steps, r.shape[1]), lambda i: (i, 0)) for r in shapes[:4]]
-    blocks.append(pl.BlockSpec(shapes[4].shape, lambda i: (0, 0)))
     gx, go, gm, gi, loss = pl.pallas_call(
-        copy_kernel, grid=(steps,), in_specs=blocks, out_specs=blocks, out_shape=shapes, name="results",
+        copy_kernel,
+        in_specs=[anywhere] * 5,
+        out_specs=[anywhere] * 5,
+        out_shape=shapes,
+        scratch_shapes=[V(shape.shape, shape.dtype) for shape in shapes] + [dma((16,))] * 2,
+        name="results",
     )(*results)
     return (loss[0], gx, gi, gm, go)
 

time: 167 us -> 156 us (0.934)
  Pallas kernels: 166 us -> 155 us
    pallas_call x1, Pallas kernels: 161 us -> 150 us  [on_device(): pl.pallas_call(functools.partial(step_kernel, words=words, total_rows=n *...]
where the time goes in v3:
time: 156 us
  Pallas kernels  155 us (99%)
    pallas_call x1, Pallas kernels, on_device(): pl.pallas_call(functools.partial(step_kernel, words=words, total_rows=n *...  150 us
    pallas_call x1, Pallas kernels, on_device(): pl.pallas_call(copy_kernel, in_specs=[anywhere] * 5, out_specs=[anywhere]...  4.82 us

profile of v3, /device:TPU:1, one launch (start us, length us, event | category | flops | bytes accessed | tf_op | source)
XLA Modules:
  0.0 156.0 jit_solution(4030637465728122738)
XLA Ops:
  0.6 150.4 %step.1 = (bf16[2048,512]{1,0:T(8,128)(2,1)}, f32[512,512]{1,0:T(8,128)}, f32[512,512]{1,0:T(8,128)}, f32[512,512]{1,0:T(8,128)}, f32[1,512]{1,0:T(1,128)}) custom-call(bf16[2048,512]{1,0:T(8,128)(2,1)} %x_in.1, bf16[512,512]{1,0:T(8,128)(2,1)} %w_in_in.1, bf16[512,512]{1,0:T(8,128)(2,1)} %w_mid_in.1, bf16[512,512]{1,0:T(8,128)(2,1)} %w_out_in.1, ...), custom_call_target="tpu_custom_call" | custom-call | tf_op jit(solution)/shard_map/step/pallas_call | solution.py:541
  151.0 4.8 %results.1 = (bf16[2048,512]{1,0:T(8,128)(2,1)}, f32[512,512]{1,0:T(8,128)}, f32[512,512]{1,0:T(8,128)}, f32[512,512]{1,0:T(8,128)}, f32[1,512]{1,0:T(1,128)}) custom-call(bf16[2048,512]{1,0:T(8,128)(2,1)} %get-tuple-element.15.refs_0_, f32[512,512]{1,0:T(8,128)} %get-tuple-element.16.refs_1_, f32[512,512]{1,0:T(8,128)} %get-tuple-element.17.refs_2_, ...), custom_call_target="tpu_custom_call" | custom-call | tf_op jit(solution)/shard_map/results/pallas_call | solution.py:551

commit v4 on v3

--- a/solution.py
+++ b/solution.py
@@ -51,12 +51,12 @@
 
 
 class Reducer:
-    def __init__(self, at, factor, given, outs, acc, pair, one, red, two, three, send, recv):
-        self.at, self.factor, self.given, self.outs = at, factor, given, outs
+    def __init__(self, at, factor, streams, given, outs, acc, pair, one, red, two, three, send, recv):
+        self.at, self.factor, self.streams, self.given, self.outs = at, factor, streams, given, outs
         self.acc, self.pair, self.one, self.red, self.two, self.three = acc, pair, one, red, two, three
         self.send, self.recv = send, recv
         self.count, self.flying, self.copies, self.own = 0, [], {}, {}
-        self.block, self.per = acc.shape[1], acc.shape[0] // len(given)
+        self.half = given[0].shape[0] // 2
         self.stages = [self.cores, self.first, self.second, self.third, self.back_second, self.back_first,
                        self.back_cores, self.finish]
 
@@ -70,85 +70,96 @@
         self.flying.append(copy)
         return copy
 
+    def matrix(self, t):
+        return self.streams[t][0]
+
+    def size(self, t, cut=1):
+        return self.streams[t][2] // cut
+
     def axis(self, t, k):
-        name = "xyz"[(t + k) % 3]
+        name = "xyz"[(self.streams[t][3] + k) % 3]
         return name, self.at[name]
 
     def others(self, name):
         return [(self.at[name] + d) % 4 for d in (2, 1, 3)]
 
     def rows_of(self, t, core, start, size):
-        blocks = self.block // size
-        return span((core * self.per + t % self.per) * blocks + start, size)
+        return span(core * (self.half // size) + self.streams[t][1] // size + start, size)
 
     def arrived(self, t):
         for copy in self.copies[t]:
             copy.wait_recv()
 
-    def stage(self, k, t):
-        self.stages[k](t)
-
     def cores(self, t):
-        core = self.at["core"]
-        away = self.rows_of(t, 1 - core, 0, self.block)
-        self.copies[t] = [self.put(self.given[t // self.per].at[away], self.pair.at[t], core=1 - core)]
+        core, size = self.at["core"], self.size(t)
+        away = self.rows_of(t, 1 - core, 0, size)
+        self.copies[t] = [
+            self.put(self.given[self.matrix(t)].at[away], self.pair.at[t, pl.ds(0, size)], core=1 - core)
+        ]
 
     def first(self, t):
         name, p = self.axis(t, 0)
         self.arrived(t)
-        kept = self.rows_of(t, self.at["core"], 0, self.block)
-        self.acc[t] = (self.given[t // self.per][kept, :] + self.pair[t]) * self.factor
-        size = self.block // 4
+        size = self.size(t)
+        kept = self.rows_of(t, self.at["core"], 0, size)
+        self.acc[t, 0:size, :] = (self.given[self.matrix(t)][kept, :] + self.pair[t, 0:size, :]) * self.factor
+        size = self.size(t, 4)
         self.copies[t] = [
-            self.put(self.acc.at[t, span(to, size)], self.one.at[t, p], **{name: to}) for to in self.others(name)
+            self.put(self.acc.at[t, span(to, size)], self.one.at[t, p, pl.ds(0, size)], **{name: to})
+            for to in self.others(name)
         ]
 
     def second(self, t):
         name, p = self.axis(t, 0)
         self.arrived(t)
-        total = self.acc[t, span(p, self.block // 4), :]
+        size = self.size(t, 4)
+        total = self.acc[t, span(p, size), :]
         for other in self.others(name):
-            total = total + self.one[t, other]
-        self.red[t] = total
+            total = total + self.one[t, other, 0:size, :]
+        self.red[t, 0:size, :] = total
         name, q = self.axis(t, 1)
-        size = self.block // 16
+        size = self.size(t, 16)
         self.copies[t] = [
-            self.put(self.red.at[t, span(to, size)], self.two.at[t, q], **{name: to}) for to in self.others(name)
+            self.put(self.red.at[t, span(to, size)], self.two.at[t, q, pl.ds(0, size)], **{name: to})
+            for to in self.others(name)
         ]
 
     def third(self, t):
         name, q = self.axis(t, 1)
         self.arrived(t)
-        total = self.red[t, span(q, self.block // 16), :]
+        size = self.size(t, 16)
+        total = self.red[t, span(q, size), :]
         for other in self.others(name):
-            total = total + self.two[t, other]
+            total = total + self.two[t, other, 0:size, :]
         name, r = self.axis(t, 2)
-        self.three[t, r] = total
-        self.copies[t] = [
-            self.put(self.three.at[t, r], self.three.at[t, r], **{name: to}) for to in self.others(name)
-        ]
+        self.three[t, r, 0:size, :] = total
+        piece = self.three.at[t, r, pl.ds(0, size)]
+        self.copies[t] = [self.put(piece, piece, **{name: to}) for to in self.others(name)]
 
     def rows(self, t, fine):
         p, q = self.axis(t, 0)[1], self.axis(t, 1)[1]
         core = self.at["core"]
-        return self.rows_of(t, core, p * 4 + q, self.block // 16) if fine else self.rows_of(t, core, p, self.block // 4)
+        return self.rows_of(t, core, p * 4 + q, self.size(t, 16)) if fine else self.rows_of(t, core, p, self.size(t, 4))
 
     def spread(self, t, rows, name):
-        piece = self.outs[t // self.per].at[rows]
+        piece = self.outs[self.matrix(t)].at[rows]
         return [self.put(piece, piece, **{name: to}) for to in self.others(name)]
 
     def back_second(self, t):
         self.arrived(t)
+        size = self.size(t, 16)
         rows = self.rows(t, True)
-        total = self.three[t, 0] + self.three[t, 1] + self.three[t, 2] + self.three[t, 3]
-        self.outs[t // self.per][rows, :] = total
+        total = self.three[t, 0, 0:size, :]
+        for slot in range(1, 4):
+            total = total + self.three[t, slot, 0:size, :]
+        self.outs[self.matrix(t)][rows, :] = total
         self.copies[t] = self.spread(t, rows, self.axis(t, 1)[0])
 
     def back_first(self, t):
         self.arrived(t)
         rows = self.rows(t, False)
         self.copies[t] = self.spread(t, rows, self.axis(t, 0)[0])
-        piece = self.outs[t // self.per].at[rows]
+        piece = self.outs[self.matrix(t)].at[rows]
         self.own[t] = self.put(piece, piece, core=1 - self.at["core"])
 
     def back_cores(self, t):
@@ -156,8 +167,8 @@
         later = [self.own[t]]
         for d, copy in zip((2, 1, 3), self.copies[t]):
             copy.wait_recv()
-            rows = self.rows_of(t, self.at["core"], (p + 4 - d) % 4, self.block // 4)
-            piece = self.outs[t // self.per].at[rows]
+            rows = self.rows_of(t, self.at["core"], (p + 4 - d) % 4, self.size(t, 4))
+            piece = self.outs[self.matrix(t)].at[rows]
             later.append(self.put(piece, piece, core=1 - self.at["core"]))
         self.copies[t] = later
 
@@ -194,7 +205,7 @@
     gx_out, go_out, gm_out, gi_out, loss_out,
     sums, x, w_in, w_mid, w_out, x_t, fh_t, hid_t, s1, s2, ind, indp, wb, w, wn, wp, own, prev, hb, hp, nb, pb,
     first_col, firstp_col, entry_col, evt, evp, idxn, logs, g, acc, pair, one, red, two, three, tally,
-    in_sem, out_sem, small_send, small_recv, w_send, w_recv, gx_sem, send, recv, *, words, total_rows, chain,
+    in_sem, out_sem, small_send, small_recv, w_send, w_recv, gx_sem, send, recv, *, words, total_rows, chain, streams,
 ):
     n, wide = x.shape[0], w_out.shape[1]
     parts, part = w.shape[0], w.shape[2]
@@ -370,7 +381,7 @@
             target[rows, :] = jnp.where(flag, 1.0 / divisors(rows), 0.0).astype(BF16)
             return 0
 
-        lax.fori_loop(0, tiles, tile, 0)
+        lax.fori_loop(0, tiles, tile, 0, unroll=2)
 
     for c in range(parts):
         cols = slice(c * part, (c + 1) * part)
@@ -404,27 +415,31 @@
             eta_ref[rows, cols] = (w[c, rows, :] * total - ind[rows, cols].astype(F32)).astype(BF16)
             return 0
 
-        lax.fori_loop(0, quarters, expose, 0)
+        lax.fori_loop(0, quarters, expose, 0, unroll=True)
         g[0, :, cols] = dot(hid_t[...], eta_ref[:, cols])
         if c < parts - 1:
             add_logs(c)
 
     mid_ref, pre_ref, gx = s2, s1, x
-    reducer = Reducer(at, total_rows ** (-0.5), [g.at[t] for t in range(3)], [sums.at[t] for t in range(3)],
+    reducer = Reducer(at, total_rows ** (-0.5), streams, [g.at[t] for t in range(3)], [sums.at[t] for t in range(3)],
                       acc, pair, one, red, two, three, send, recv)
     counted = Tally(reducer, tally)
 
     outs = [pltpu.make_async_copy(sums.at[t], out, out_sem.at[t]) for t, out in enumerate((go_out, gm_out, gi_out))]
 
+    def advance(t, k):
+        if 0 <= k < len(reducer.stages):
+            for v, stream in enumerate(streams):
+                if stream[0] == t:
+                    reducer.stages[k](v)
+            if k == len(reducer.stages) - 1:
+                outs[t].start()
+
     def turn(k):
         for t in range(2, -1, -1):
-            if 0 <= k - t < len(reducer.stages):
-                for v in range(reducer.per):
-                    reducer.stage(k - t, t * reducer.per + v)
-                if k - t == len(reducer.stages) - 1:
-                    outs[t].start()
-
-    turn(0)
+            advance(t, k - t)
+
+    advance(0, 0)
 
     def middle(i, _):
         rows = span(i, Q)
@@ -432,9 +447,13 @@
         mid_ref[rows, :] = mid_grad.astype(BF16)
         return 0
 
-    lax.fori_loop(0, quarters, middle, 0)
-    g[1] = dot(fh_t[...], mid_ref[...])
-    turn(1)
+    lax.fori_loop(0, quarters, middle, 0, unroll=True)
+    advance(0, 1)
+    half = g.shape[1] // 2
+    away, kept = span(1 - at["core"], half), span(at["core"], half)
+    g[1, away, :] = dot(fh_t[away, :], mid_ref[...])
+    advance(1, 0)
+    g[1, kept, :] = dot(fh_t[kept, :], mid_ref[...])
 
     def inner(i, _):
         rows = span(i, Q)
@@ -442,29 +461,32 @@
         pre_ref[rows, :] = pre_grad.astype(BF16)
         return 0
 
-    lax.fori_loop(0, quarters, inner, 0)
-    g[2] = dot(x_t[...], pre_ref[...])
-    turn(2)
-    add_logs(parts - 1)
-    counted.send(0, logs[...] / total_rows)
+    lax.fori_loop(0, quarters, inner, 0, unroll=True)
+    advance(1, 1)
+    g[2, away, :] = dot(x_t[away, :], pre_ref[...])
+    advance(2, 0)
+    g[2, kept, :] = dot(x_t[kept, :], pre_ref[...])
+    advance(0, 2)
 
     def last(i, _):
         rows = span(i, Q)
         gx[rows, :] = dot(pre_ref[rows, :], w_in[...], ((1,), (1,))).astype(BF16)
         return 0
 
-    turn(3)
-    counted.send(1, counted.total(0))
+    advance(2, 1)
+    add_logs(parts - 1)
+    counted.send(0, logs[...] / total_rows)
+    advance(1, 2)
+    advance(0, 3)
     lax.fori_loop(0, quarters, last, 0)
     gx_copy = pltpu.make_async_copy(gx, gx_out, gx_sem)
     gx_copy.start()
-    turn(4)
-    counted.send(2, counted.total(1))
-    turn(5)
-    counted.send(3, counted.total(2))
-    turn(6)
+    for k in range(4, 7):
+        turn(k)
+        counted.send(k - 3, counted.total(k - 4))
+    turn(7)
     loss_out[...] = jnp.sum(counted.total(3), axis=0, keepdims=True)
-    for k in range(7, len(reducer.stages) + 2):
+    for k in range(8, len(reducer.stages) + 2):
         turn(k)
     reducer.drain()
     gx_copy.wait()
@@ -518,9 +540,11 @@
     bit = jnp.asarray((np.arange(wide) % WORD_BITS)[None, :].astype(np.int32))
 
     m = 3
-    per = 2
-    streams, block = m * per, hidden_width // 2 // per
-    messages = streams * 20 + 10
+    half = hidden_width // 2
+    large = half // 2
+    streams = tuple((t, v * large, large, (2 * t + v) % 3) for t in range(m) for v in range(2))
+    many = len(streams)
+    messages = many * 20 + 10
     V = pltpu.VMEM
     dma = pltpu.SemaphoreType.DMA
     by_rows, by_columns, square = V((n, wide), BF16), V((wide, n), BF16), V((wide, wide), BF16)
@@ -529,9 +553,9 @@
         + [V((parts, n, part), F32)] * 5
         + [V((n, part), BF16)] * 2 + [V((Q, part), BF16)] * 2 + [V((n, 128), I32)] * 3
         + [V((deep, n), I32)] * 2 + [V((8, n), I32), V((8, wide), F32), V((m, hidden_width, wide), F32)]
-        + [V((streams, block, wide), F32)] * 2
-        + [V((streams, 4, block // 4, wide), F32), V((streams, block // 4, wide), F32)]
-        + [V((streams, 4, block // 16, wide), F32)] * 2 + [V((4, 4, 8, wide), F32)]
+        + [V((many, large, wide), F32)] * 2
+        + [V((many, 4, large // 4, wide), F32), V((many, large // 4, wide), F32)]
+        + [V((many, 4, large // 16, wide), F32)] * 2 + [V((4, 4, 8, wide), F32)]
         + [dma((4,)), dma((m,))] + [dma((2,))] * 2 + [dma((2, parts, n // T))] * 2 + [dma, dma((messages,)), dma((messages,))]
     )
     vmem = pl.BlockSpec(memory_space=V)
@@ -539,7 +563,7 @@
     grad = jax.ShapeDtypeStruct((hidden_width, wide), F32)
     shapes = [jax.ShapeDtypeStruct((n, width), BF16), grad, grad, grad, jax.ShapeDtypeStruct((1, wide), F32)]
     results = pl.pallas_call(
-        functools.partial(step_kernel, words=words, total_rows=n * chain * strata, chain=chain),
+        functools.partial(step_kernel, words=words, total_rows=n * chain * strata, chain=chain, streams=streams),
         in_specs=[anywhere] * 4 + [vmem] * 5,
         out_specs=[anywhere] * 4 + [vmem],
         out_shape=shapes,

time: 156 us -> 155 us (level)
  no operation moved by 1% of the time
where the time goes in v4:
time: 155 us
  Pallas kernels  154 us (99%)
    pallas_call x1, Pallas kernels, on_device(): pl.pallas_call(functools.partial(step_kernel, words=words, total_rows=n *...  149 us
    pallas_call x1, Pallas kernels, on_device(): pl.pallas_call(copy_kernel, in_specs=[anywhere] * 5, out_specs=[anywhere]...  4.82 us

profile of v4, /device:TPU:1, one launch (start us, length us, event | category | flops | bytes accessed | tf_op | source)
XLA Modules:
  0.0 154.6 jit_solution(12868983303348729317)
XLA Ops:
  0.6 149.0 %step.1 = (bf16[2048,512]{1,0:T(8,128)(2,1)}, f32[512,512]{1,0:T(8,128)}, f32[512,512]{1,0:T(8,128)}, f32[512,512]{1,0:T(8,128)}, f32[1,512]{1,0:T(1,128)}) custom-call(bf16[2048,512]{1,0:T(8,128)(2,1)} %x_in.1, bf16[512,512]{1,0:T(8,128)(2,1)} %w_in_in.1, bf16[512,512]{1,0:T(8,128)(2,1)} %w_mid_in.1, bf16[512,512]{1,0:T(8,128)(2,1)} %w_out_in.1, ...), custom_call_target="tpu_custom_call" | custom-call | tf_op jit(solution)/shard_map/step/pallas_call | solution.py:565
  149.6 4.8 %results.1 = (bf16[2048,512]{1,0:T(8,128)(2,1)}, f32[512,512]{1,0:T(8,128)}, f32[512,512]{1,0:T(8,128)}, f32[512,512]{1,0:T(8,128)}, f32[1,512]{1,0:T(1,128)}) custom-call(bf16[2048,512]{1,0:T(8,128)(2,1)} %get-tuple-element.15.refs_0_, f32[512,512]{1,0:T(8,128)} %get-tuple-element.16.refs_1_, f32[512,512]{1,0:T(8,128)} %get-tuple-element.17.refs_2_, ...), custom_call_target="tpu_custom_call" | custom-call | tf_op jit(solution)/shard_map/results/pallas_call | solution.py:575

commit v5 on v4

--- a/solution.py
+++ b/solution.py
@@ -201,9 +201,9 @@
 
 
 def step_kernel(
-    x_in, w_in_in, w_mid_in, w_out_in, events, tie, entry_in, spread, bit,
+    x_in, w_in_in, w_mid_in, w_out_in, events_in, tie_in, entry_in, spread_in, bit_in,
     gx_out, go_out, gm_out, gi_out, loss_out,
-    sums, x, w_in, w_mid, w_out, x_t, fh_t, hid_t, s1, s2, ind, indp, wb, w, wn, wp, own, prev, hb, hp, nb, pb,
+    events, tie, entry_rows, spread, bit, sums, x, w_in, w_mid, w_out, x_t, fh_t, hid_t, s1, s2, ind, indp, wb, w, wn, wp, own, prev, hb, hp, nb, pb,
     first_col, firstp_col, entry_col, evt, evp, idxn, logs, g, acc, pair, one, red, two, three, tally,
     in_sem, out_sem, small_send, small_recv, w_send, w_recv, gx_sem, send, recv, *, words, total_rows, chain, streams,
 ):
@@ -223,13 +223,17 @@
         pl.semaphore_signal(barrier, inc=1, device_id=friend, device_id_type=MESH)
     loads = [
         pltpu.make_async_copy(source, target, in_sem.at[k])
-        for k, (source, target) in enumerate(((x_in, x), (w_in_in, w_in), (w_mid_in, w_mid), (w_out_in, w_out)))
+        for k, (source, target) in enumerate((
+            (events_in, events), (tie_in, tie), (entry_in, entry_rows), (w_in_in, w_in), (x_in, x),
+            (w_mid_in, w_mid), (w_out_in, w_out), (spread_in, spread), (bit_in, bit)))
     ]
     for load in loads:
         load.start()
+    for load in loads[:3]:
+        load.wait()
     evt[0:words, :] = events[...]
     evt[words : words + 1, :] = tie[...] - me * n
-    evt[words + 1 : words + 2, :] = entry_in[...] - me * n + n
+    evt[words + 1 : words + 2, :] = entry_rows[...] - me * n + n
     evt[words + 2 :, :] = jnp.zeros((evt.shape[0] - words - 2, n), I32)
     pl.semaphore_wait(barrier, len(friends))
 
@@ -252,7 +256,7 @@
         return remote(w.at[c, rows], wp.at[c, rows], w_send.at[1, c, r], w_recv.at[1, c, r], right)
 
     logs[...] = jnp.zeros_like(logs)
-    for load in loads:
+    for load in loads[3:]:
         load.wait()
 
     def forward(r, _):
@@ -509,7 +513,7 @@
     sources, targets, buffers, sem_in, sem_out = refs[:m], refs[m : 2 * m], refs[2 * m : 3 * m], refs[-2], refs[-1]
     reads, writes = [], []
     for source, target, buffer in zip(sources, targets, buffers):
-        pieces = max(source.shape[0] // 256, 1) if source.dtype == F32 else source.shape[0] // 512
+        pieces = max(source.shape[0] // 128, 1) if source.dtype == F32 else source.shape[0] // 256
         size = source.shape[0] // pieces
         for k in range(pieces):
             at = pl.ds(k * size, size)
@@ -549,14 +553,15 @@
     dma = pltpu.SemaphoreType.DMA
     by_rows, by_columns, square = V((n, wide), BF16), V((wide, n), BF16), V((wide, wide), BF16)
     scratch = (
-        [V((m, hidden_width, wide), F32), by_rows] + [square] * 3 + [by_columns] * 3 + [by_rows] * 5
+        [V((words, n), I32), V((1, n), I32), V((1, n), I32), V(spread.shape, BF16), V(bit.shape, I32)]
+        + [V((m, hidden_width, wide), F32), by_rows] + [square] * 3 + [by_columns] * 3 + [by_rows] * 5
         + [V((parts, n, part), F32)] * 5
         + [V((n, part), BF16)] * 2 + [V((Q, part), BF16)] * 2 + [V((n, 128), I32)] * 3
         + [V((deep, n), I32)] * 2 + [V((8, n), I32), V((8, wide), F32), V((m, hidden_width, wide), F32)]
         + [V((many, large, wide), F32)] * 2
         + [V((many, 4, large // 4, wide), F32), V((many, large // 4, wide), F32)]
         + [V((many, 4, large // 16, wide), F32)] * 2 + [V((4, 4, 8, wide), F32)]
-        + [dma((4,)), dma((m,))] + [dma((2,))] * 2 + [dma((2, parts, n // T))] * 2 + [dma, dma((messages,)), dma((messages,))]
+        + [dma((9,)), dma((m,))] + [dma((2,))] * 2 + [dma((2, parts, n // T))] * 2 + [dma, dma((messages,)), dma((messages,))]
     )
     vmem = pl.BlockSpec(memory_space=V)
     anywhere = pl.BlockSpec(memory_space=pl.ANY)
@@ -564,7 +569,7 @@
     shapes = [jax.ShapeDtypeStruct((n, width), BF16), grad, grad, grad, jax.ShapeDtypeStruct((1, wide), F32)]
     results = pl.pallas_call(
         functools.partial(step_kernel, words=words, total_rows=n * chain * strata, chain=chain, streams=streams),
-        in_specs=[anywhere] * 4 + [vmem] * 5,
+        in_specs=[anywhere] * 9,
         out_specs=[anywhere] * 4 + [vmem],
         out_shape=shapes,
         scratch_shapes=scratch,
@@ -577,7 +582,7 @@
         in_specs=[anywhere] * 5,
         out_specs=[anywhere] * 5,
         out_shape=shapes,
-        scratch_shapes=[V(shape.shape, shape.dtype) for shape in shapes] + [dma((16,))] * 2,
+        scratch_shapes=[V(shape.shape, shape.dtype) for shape in shapes] + [dma((24,))] * 2,
         name="results",
     )(*results)
     return (loss[0], gx, gi, gm, go)

time: 155 us -> 154 us (level)
  no operation moved by 1% of the time
where the time goes in v5:
time: 154 us
  Pallas kernels  153 us (99%)
    pallas_call x1, Pallas kernels, on_device(): pl.pallas_call(functools.partial(step_kernel, words=words, total_rows=n *...  148 us
    pallas_call x1, Pallas kernels, on_device(): pl.pallas_call(copy_kernel, in_specs=[anywhere] * 5, out_specs=[anywhere]...  5.09 us

profile of v5, /device:TPU:1, one launch (start us, length us, event | category | flops | bytes accessed | tf_op | source)
XLA Modules:
  0.0 154.1 jit_solution(16820876996686648617)
XLA Ops:
  0.6 148.2 %step.1 = (bf16[2048,512]{1,0:T(8,128)(2,1)}, f32[512,512]{1,0:T(8,128)}, f32[512,512]{1,0:T(8,128)}, f32[512,512]{1,0:T(8,128)}, f32[1,512]{1,0:T(1,128)}) custom-call(bf16[2048,512]{1,0:T(8,128)(2,1)} %x_in.1, bf16[512,512]{1,0:T(8,128)(2,1)} %w_in_in.1, bf16[512,512]{1,0:T(8,128)(2,1)} %w_mid_in.1, bf16[512,512]{1,0:T(8,128)(2,1)} %w_out_in.1, ...), custom_call_target="tpu_custom_call" | custom-call | tf_op jit(solution)/shard_map/step/pallas_call | solution.py:570
  148.8 5.1 %results.1 = (bf16[2048,512]{1,0:T(8,128)(2,1)}, f32[512,512]{1,0:T(8,128)}, f32[512,512]{1,0:T(8,128)}, f32[512,512]{1,0:T(8,128)}, f32[1,512]{1,0:T(1,128)}) custom-call(bf16[2048,512]{1,0:T(8,128)(2,1)} %get-tuple-element.15.refs_0_, f32[512,512]{1,0:T(8,128)} %get-tuple-element.16.refs_1_, f32[512,512]{1,0:T(8,128)} %get-tuple-element.17.refs_2_, ...), custom_call_target="tpu_custom_call" | custom-call | tf_op jit(solution)/shard_map/results/pallas_call | solution.py:580
